TPU v7x, 32 devices: a whole 2x2x4 slice. The times are simulated.
32 devices in a mesh: group: 2 (over x), lev: 2 (over core), row: 8 (over z, y).
Axes of the slice: x: 2, y: 2, z: 4, core: 2. Of those that a mesh axis runs over, the one named last changes fastest.
Arguments:
- fields: bfloat16 [6, 90, 64, 1024], P('group', 'lev', 'row'), parts along dimension 0, may hold values from -6 to 6
- vertical_modes: bfloat16 [8, 90, 64, 1024], P(None, 'lev', 'row'), may hold values from -0.625 to 0.625
- diffusivity: float32 [64, 1024], P('row'), may hold values from 0.05 to 0.245
- land_mask: int32 [64, 1024], P('row'), may hold values 0 or 1
- wet_levels: int32 [64, 1024], P('row'), may hold values from 1 to 90
Outputs:
- filtered: bfloat16 [6, 90, 64, 1024], P('group', 'lev', 'row'), parts along dimension 0
- modal_flux: float32 [6, 8, 64, 1024], P('group', None, 'row', 'lev'), parts along dimension 0
There are 2 independent parts, one for each index of `group`. A program takes and returns all parts, laid end to end along the dimension named above; an argument that names none is the same for every part. Nothing has to cross between parts.
All inputs are finite; a program needn't handle non-finite values. No bound on the sum of `land_mask` on one device may be relied on, other than what follows from the above.
Results may differ from a plain program's by a relative error of at most 0.00092.
Values may be sent and summed in bfloat16 or wider, within the bound.
No kernel may reach another device: no remote copies, remote signals or barrier semaphores. Data moves between devices by JAX's collectives and lax.ppermute only.
A program may use at most 192 MiB of HBM per device.

v0:
```python
import jax
import jax.numpy as jnp
from jax import lax
from jax.sharding import PartitionSpec as P

ITERS = 10


def extended_2(value, sides, width):
    for axis, dim in sides:
        size, length = (lax.axis_size(axis), value.shape[dim])
        up = [(i, (i + 1) % size) for i in range(size - 1)]
        down = [(j, i) for i, j in up]
        last = lax.slice_in_dim(value, length - width, length, axis=dim)
        first = lax.slice_in_dim(value, 0, width, axis=dim)
        before = lax.ppermute(last, axis, up)
        after = lax.ppermute(first, axis, down)
        value = jnp.concatenate([before, value, after], axis=dim)
    return value


def face_weights(diffusivity, wet_depth, lev_start, lev_count):
    level_index = lev_start + jnp.arange(lev_count, dtype=jnp.float32)
    wet_cells = (level_index[:, None, None] < wet_depth[None]).astype(jnp.float32)
    east_weight = (
        0.5
        * (diffusivity[:, :-1] + diffusivity[:, 1:])[None]
        * wet_cells[:, :, :-1]
        * wet_cells[:, :, 1:]
    )
    east_weight = jnp.pad(east_weight, ((0, 0), (0, 0), (0, 1)))
    north_weight = (
        0.5 * (diffusivity[:-1] + diffusivity[1:])[None] * wet_cells[:, :-1] * wet_cells[:, 1:]
    )
    north_weight = jnp.pad(north_weight, ((0, 0), (0, 1), (0, 0)))
    return (east_weight, north_weight)


def smooth(current, east_weight, north_weight):
    east_flux = east_weight * (jnp.roll(current, -1, 3) - current)
    north_flux = north_weight * (jnp.roll(current, -1, 2) - current)
    east_side = east_flux - jnp.roll(east_flux, 1, 3)
    north_side = north_flux - jnp.roll(north_flux, 1, 2)
    return current + east_side + north_side


def project(vertical_modes, rounded):
    return jnp.einsum(
        "klrc,flrc->fkrc", vertical_modes, rounded, preferred_element_type=jnp.float32
    )


def per_device(fields, vertical_modes, diffusivity, land_mask, wet_levels):
    lev_count = fields.shape[1]
    strip_rows = fields.shape[2]
    lev_start = (lax.axis_index("lev") * lev_count).astype(jnp.float32)
    wet_depth = (land_mask * wet_levels).astype(jnp.float32)
    statics = extended_2(jnp.stack([diffusivity, wet_depth]), (("row", 1),), 5)
    current = fields.astype(jnp.float32)
    east_weight, north_weight = face_weights(
        statics[0, 4 : strip_rows + 6], statics[1, 4 : strip_rows + 6], lev_start, lev_count
    )

    def one_step(step_index, present):
        extended = extended_2(present, (("row", 2),), 1)
        return smooth(extended, east_weight, north_weight)[:, :, 1 : strip_rows + 1]

    current = lax.fori_loop(0, ITERS, one_step, current)
    rounded = current.astype(jnp.bfloat16)
    amplitude = lax.psum_scatter(
        project(vertical_modes, rounded), "lev", scatter_dimension=3, tiled=True
    )
    modal_flux = jnp.stack(
        [
            amplitude[0] * amplitude[2],
            amplitude[1] * amplitude[2],
            0.5 * (amplitude[0] * amplitude[0] + amplitude[1] * amplitude[1]),
        ]
    )
    return (rounded, modal_flux)


def solution(mesh):
    placed = (
        P("group", "lev", "row", None),
        P(None, "lev", "row", None),
        P("row", None),
        P("row", None),
        P("row", None),
    )
    return jax.shard_map(
        per_device,
        mesh=mesh,
        in_specs=placed,
        out_specs=(P("group", "lev", "row", None), P("group", None, "row", "lev")),
        check_vma=False,
    )
```

profile of v0, /device:TPU:11, one launch (start us, length us, event | category | flops | bytes accessed | tf_op | source)
XLA Modules:
  0.0 883.5 jit_solution(4433715931043792953)
XLA Ops:
  38.9 758.7 %while.10 = (s32[]{:T(128)}, f32[3,45,8,1024]{3,2,1,0:T(8,128)}, f32[45,10,1024]{2,1,0:T(8,128)}, f32[45,10,1024]{2,1,0:T(8,128)}, s32[]{:T(128)}) while((s32[]{:T(128)}, f32[3,45,8,1024]{3,2,1,0:T(8,128)}, f32[45,10,1024]{2,1,0:T(8,128)}, f32[45,10,1024]{2,1,0:T(8,128)}, s32[]{:T(128)}) %tuple.35), condition=%wide.region_1.2_spmd, body=%wide.region_0.1_spmd.sunk | while | flops 21841920 | bytes 164055888 | solution.py:68
  49.0 21.2 %collective-permute-done = f32[3,45,1,1024]{3,2,1,0:T(1,128)S(1)} collective-permute-done((f32[3,45,1,1024]{3,2,1,0:T(1,128)S(1)}, f32[3,45,1,1024]{3,2,1,0:T(1,128)S(1)}, u32[]{:S(2)}, u32[]{:S(2)}) %collective-permute-start) | collective-permute-done | bytes 552992 | tf_op jit(solution)/shard_map/while/body/eval_jaxpr/ppermute | solution.py:17
  96.0 17.1 %fusion.18 = f32[3,45,8,1024]{3,2,1,0:T(8,128)} fusion(f32[3,45,10,1024]{3,2,1,0:T(8,128)} %copy-done.2, f32[3,45,10,1024]{3,2,1,0:T(8,128)} %copy-done, f32[3,45,9,1024]{3,2,1,0:T(8,128)} %bitcast.20, f32[3,45,1,1024]{3,2,1,0:T(1,128)S(1)} %slice.173, f32[3,45,10,1024]{3,2,1,0:T(8,128)} %copy-done.1, f32[3,45,10,1023]{3,2,1,0:T(8,128)} %bitcast.19, ...), kind=kLoop, calls=%fused_computation.6.clone.1 | loop fusion | flops 6635520 | bytes 28753920 | tf_op jit(solution)/shard_map/while/body/eval_jaxpr/add | solution.py:44
  123.9 21.8 %collective-permute-done = f32[3,45,1,1024]{3,2,1,0:T(1,128)S(1)} collective-permute-done((f32[3,45,1,1024]{3,2,1,0:T(1,128)S(1)}, f32[3,45,1,1024]{3,2,1,0:T(1,128)S(1)}, u32[]{:S(2)}, u32[]{:S(2)}) %collective-permute-start) | collective-permute-done | bytes 552992 | tf_op jit(solution)/shard_map/while/body/eval_jaxpr/ppermute | solution.py:17
  172.0 17.1 %fusion.18 = f32[3,45,8,1024]{3,2,1,0:T(8,128)} fusion(f32[3,45,10,1024]{3,2,1,0:T(8,128)} %copy-done.2, f32[3,45,10,1024]{3,2,1,0:T(8,128)} %copy-done, f32[3,45,9,1024]{3,2,1,0:T(8,128)} %bitcast.20, f32[3,45,1,1024]{3,2,1,0:T(1,128)S(1)} %slice.173, f32[3,45,10,1024]{3,2,1,0:T(8,128)} %copy-done.1, f32[3,45,10,1023]{3,2,1,0:T(8,128)} %bitcast.19, ...), kind=kLoop, calls=%fused_computation.6.clone.1 | loop fusion | flops 6635520 | bytes 28753920 | tf_op jit(solution)/shard_map/while/body/eval_jaxpr/add | solution.py:44
  200.0 22.4 %collective-permute-done = f32[3,45,1,1024]{3,2,1,0:T(1,128)S(1)} collective-permute-done((f32[3,45,1,1024]{3,2,1,0:T(1,128)S(1)}, f32[3,45,1,1024]{3,2,1,0:T(1,128)S(1)}, u32[]{:S(2)}, u32[]{:S(2)}) %collective-permute-start) | collective-permute-done | bytes 552992 | tf_op jit(solution)/shard_map/while/body/eval_jaxpr/ppermute | solution.py:17
  248.1 17.1 %fusion.18 = f32[3,45,8,1024]{3,2,1,0:T(8,128)} fusion(f32[3,45,10,1024]{3,2,1,0:T(8,128)} %copy-done.2, f32[3,45,10,1024]{3,2,1,0:T(8,128)} %copy-done, f32[3,45,9,1024]{3,2,1,0:T(8,128)} %bitcast.20, f32[3,45,1,1024]{3,2,1,0:T(1,128)S(1)} %slice.173, f32[3,45,10,1024]{3,2,1,0:T(8,128)} %copy-done.1, f32[3,45,10,1023]{3,2,1,0:T(8,128)} %bitcast.19, ...), kind=kLoop, calls=%fused_computation.6.clone.1 | loop fusion | flops 6635520 | bytes 28753920 | tf_op jit(solution)/shard_map/while/body/eval_jaxpr/add | solution.py:44
  276.1 22.4 %collective-permute-done = f32[3,45,1,1024]{3,2,1,0:T(1,128)S(1)} collective-permute-done((f32[3,45,1,1024]{3,2,1,0:T(1,128)S(1)}, f32[3,45,1,1024]{3,2,1,0:T(1,128)S(1)}, u32[]{:S(2)}, u32[]{:S(2)}) %collective-permute-start) | collective-permute-done | bytes 552992 | tf_op jit(solution)/shard_map/while/body/eval_jaxpr/ppermute | solution.py:17
  324.1 17.1 %fusion.18 = f32[3,45,8,1024]{3,2,1,0:T(8,128)} fusion(f32[3,45,10,1024]{3,2,1,0:T(8,128)} %copy-done.2, f32[3,45,10,1024]{3,2,1,0:T(8,128)} %copy-done, f32[3,45,9,1024]{3,2,1,0:T(8,128)} %bitcast.20, f32[3,45,1,1024]{3,2,1,0:T(1,128)S(1)} %slice.173, f32[3,45,10,1024]{3,2,1,0:T(8,128)} %copy-done.1, f32[3,45,10,1023]{3,2,1,0:T(8,128)} %bitcast.19, ...), kind=kLoop, calls=%fused_computation.6.clone.1 | loop fusion | flops 6635520 | bytes 28753920 | tf_op jit(solution)/shard_map/while/body/eval_jaxpr/add | solution.py:44
  352.1 22.4 %collective-permute-done = f32[3,45,1,1024]{3,2,1,0:T(1,128)S(1)} collective-permute-done((f32[3,45,1,1024]{3,2,1,0:T(1,128)S(1)}, f32[3,45,1,1024]{3,2,1,0:T(1,128)S(1)}, u32[]{:S(2)}, u32[]{:S(2)}) %collective-permute-start) | collective-permute-done | bytes 552992 | tf_op jit(solution)/shard_map/while/body/eval_jaxpr/ppermute | solution.py:17
  400.2 17.1 %fusion.18 = f32[3,45,8,1024]{3,2,1,0:T(8,128)} fusion(f32[3,45,10,1024]{3,2,1,0:T(8,128)} %copy-done.2, f32[3,45,10,1024]{3,2,1,0:T(8,128)} %copy-done, f32[3,45,9,1024]{3,2,1,0:T(8,128)} %bitcast.20, f32[3,45,1,1024]{3,2,1,0:T(1,128)S(1)} %slice.173, f32[3,45,10,1024]{3,2,1,0:T(8,128)} %copy-done.1, f32[3,45,10,1023]{3,2,1,0:T(8,128)} %bitcast.19, ...), kind=kLoop, calls=%fused_computation.6.clone.1 | loop fusion | flops 6635520 | bytes 28753920 | tf_op jit(solution)/shard_map/while/body/eval_jaxpr/add | solution.py:44
  428.2 22.4 %collective-permute-done = f32[3,45,1,1024]{3,2,1,0:T(1,128)S(1)} collective-permute-done((f32[3,45,1,1024]{3,2,1,0:T(1,128)S(1)}, f32[3,45,1,1024]{3,2,1,0:T(1,128)S(1)}, u32[]{:S(2)}, u32[]{:S(2)}) %collective-permute-start) | collective-permute-done | bytes 552992 | tf_op jit(solution)/shard_map/while/body/eval_jaxpr/ppermute | solution.py:17
  476.2 17.1 %fusion.18 = f32[3,45,8,1024]{3,2,1,0:T(8,128)} fusion(f32[3,45,10,1024]{3,2,1,0:T(8,128)} %copy-done.2, f32[3,45,10,1024]{3,2,1,0:T(8,128)} %copy-done, f32[3,45,9,1024]{3,2,1,0:T(8,128)} %bitcast.20, f32[3,45,1,1024]{3,2,1,0:T(1,128)S(1)} %slice.173, f32[3,45,10,1024]{3,2,1,0:T(8,128)} %copy-done.1, f32[3,45,10,1023]{3,2,1,0:T(8,128)} %bitcast.19, ...), kind=kLoop, calls=%fused_computation.6.clone.1 | loop fusion | flops 6635520 | bytes 28753920 | tf_op jit(solution)/shard_map/while/body/eval_jaxpr/add | solution.py:44
  504.2 22.4 %collective-permute-done = f32[3,45,1,1024]{3,2,1,0:T(1,128)S(1)} collective-permute-done((f32[3,45,1,1024]{3,2,1,0:T(1,128)S(1)}, f32[3,45,1,1024]{3,2,1,0:T(1,128)S(1)}, u32[]{:S(2)}, u32[]{:S(2)}) %collective-permute-start) | collective-permute-done | bytes 552992 | tf_op jit(solution)/shard_map/while/body/eval_jaxpr/ppermute | solution.py:17
  552.3 17.1 %fusion.18 = f32[3,45,8,1024]{3,2,1,0:T(8,128)} fusion(f32[3,45,10,1024]{3,2,1,0:T(8,128)} %copy-done.2, f32[3,45,10,1024]{3,2,1,0:T(8,128)} %copy-done, f32[3,45,9,1024]{3,2,1,0:T(8,128)} %bitcast.20, f32[3,45,1,1024]{3,2,1,0:T(1,128)S(1)} %slice.173, f32[3,45,10,1024]{3,2,1,0:T(8,128)} %copy-done.1, f32[3,45,10,1023]{3,2,1,0:T(8,128)} %bitcast.19, ...), kind=kLoop, calls=%fused_computation.6.clone.1 | loop fusion | flops 6635520 | bytes 28753920 | tf_op jit(solution)/shard_map/while/body/eval_jaxpr/add | solution.py:44
  580.3 22.4 %collective-permute-done = f32[3,45,1,1024]{3,2,1,0:T(1,128)S(1)} collective-permute-done((f32[3,45,1,1024]{3,2,1,0:T(1,128)S(1)}, f32[3,45,1,1024]{3,2,1,0:T(1,128)S(1)}, u32[]{:S(2)}, u32[]{:S(2)}) %collective-permute-start) | collective-permute-done | bytes 552992 | tf_op jit(solution)/shard_map/while/body/eval_jaxpr/ppermute | solution.py:17
  628.3 17.1 %fusion.18 = f32[3,45,8,1024]{3,2,1,0:T(8,128)} fusion(f32[3,45,10,1024]{3,2,1,0:T(8,128)} %copy-done.2, f32[3,45,10,1024]{3,2,1,0:T(8,128)} %copy-done, f32[3,45,9,1024]{3,2,1,0:T(8,128)} %bitcast.20, f32[3,45,1,1024]{3,2,1,0:T(1,128)S(1)} %slice.173, f32[3,45,10,1024]{3,2,1,0:T(8,128)} %copy-done.1, f32[3,45,10,1023]{3,2,1,0:T(8,128)} %bitcast.19, ...), kind=kLoop, calls=%fused_computation.6.clone.1 | loop fusion | flops 6635520 | bytes 28753920 | tf_op jit(solution)/shard_map/while/body/eval_jaxpr/add | solution.py:44
  656.3 22.4 %collective-permute-done = f32[3,45,1,1024]{3,2,1,0:T(1,128)S(1)} collective-permute-done((f32[3,45,1,1024]{3,2,1,0:T(1,128)S(1)}, f32[3,45,1,1024]{3,2,1,0:T(1,128)S(1)}, u32[]{:S(2)}, u32[]{:S(2)}) %collective-permute-start) | collective-permute-done | bytes 552992 | tf_op jit(solution)/shard_map/while/body/eval_jaxpr/ppermute | solution.py:17
  704.4 17.1 %fusion.18 = f32[3,45,8,1024]{3,2,1,0:T(8,128)} fusion(f32[3,45,10,1024]{3,2,1,0:T(8,128)} %copy-done.2, f32[3,45,10,1024]{3,2,1,0:T(8,128)} %copy-done, f32[3,45,9,1024]{3,2,1,0:T(8,128)} %bitcast.20, f32[3,45,1,1024]{3,2,1,0:T(1,128)S(1)} %slice.173, f32[3,45,10,1024]{3,2,1,0:T(8,128)} %copy-done.1, f32[3,45,10,1023]{3,2,1,0:T(8,128)} %bitcast.19, ...), kind=kLoop, calls=%fused_computation.6.clone.1 | loop fusion | flops 6635520 | bytes 28753920 | tf_op jit(solution)/shard_map/while/body/eval_jaxpr/add | solution.py:44
  732.4 22.4 %collective-permute-done = f32[3,45,1,1024]{3,2,1,0:T(1,128)S(1)} collective-permute-done((f32[3,45,1,1024]{3,2,1,0:T(1,128)S(1)}, f32[3,45,1,1024]{3,2,1,0:T(1,128)S(1)}, u32[]{:S(2)}, u32[]{:S(2)}) %collective-permute-start) | collective-permute-done | bytes 552992 | tf_op jit(solution)/shard_map/while/body/eval_jaxpr/ppermute | solution.py:17
  780.5 17.1 %fusion.18 = f32[3,45,8,1024]{3,2,1,0:T(8,128)} fusion(f32[3,45,10,1024]{3,2,1,0:T(8,128)} %copy-done.2, f32[3,45,10,1024]{3,2,1,0:T(8,128)} %copy-done, f32[3,45,9,1024]{3,2,1,0:T(8,128)} %bitcast.20, f32[3,45,1,1024]{3,2,1,0:T(1,128)S(1)} %slice.173, f32[3,45,10,1024]{3,2,1,0:T(8,128)} %copy-done.1, f32[3,45,10,1023]{3,2,1,0:T(8,128)} %bitcast.19, ...), kind=kLoop, calls=%fused_computation.6.clone.1 | loop fusion | flops 6635520 | bytes 28753920 | tf_op jit(solution)/shard_map/while/body/eval_jaxpr/add | solution.py:44
  807.1 17.6 %convolution_bitcast_fusion = f32[3,8,8,1024]{1,0,3,2:T(4,128)} fusion(bf16[3,45,8,1024]{1,0,3,2:T(4,128)(2,1)} %copy.22, bf16[8,45,8,1024]{1,0,3,2:T(8,128)(2,1)} %copy.23), kind=kOutput, calls=%fused_computation.11 | convolution fusion | flops 17694720 | bytes 8896512 | tf_op jit(solution)/shard_map/klrc,flrc->fkrc/dot_general | solution.py:48
  824.6 17.6 %copy.24 = f32[3,8,8,1024]{2,1,0,3:T(8,128)} copy(f32[3,8,8,1024]{1,0,3,2:T(4,128)} %convolution_bitcast_fusion) | data formatting | bytes 1572864 | tf_op jit(solution)/shard_map/klrc,flrc->fkrc/transpose | solution.py:48
  842.3 23.3 %reduce-scatter.2.cloned.1.call-done = f32[3,8,8,512]{2,1,0,3:T(8,128)} async-done(((f32[3,8,8,1024]{2,1,0,3:T(8,128)}), f32[3,8,8,512]{2,1,0,3:T(8,128)}) %reduce-scatter.2.cloned.1.call-update) | async-done | bytes 393232 | tf_op jit(solution)/shard_map/reduce_scatter | solution.py:70
  (241 shorter events, 416.6 us)
Async XLA Ops:
  7.2 858.4 %reduce-scatter.2.cloned.1.call-start = ((), (), s32[]{:S(2)}) async-start(), calls=%async_computation.1 | async-start | bytes 18874368 | tf_op jit(solution)/shard_map/reduce_scatter | solution.py:70
  8.8 23.8 %collective-permute-start.2 = (f32[2,5,1024]{2,1,0:T(8,128)S(1)}, f32[2,5,1024]{2,1,0:T(8,128)S(1)}, u32[]{:S(2)}, u32[]{:S(2)}) collective-permute-start(f32[2,5,1024]{2,1,0:T(8,128)S(1)} %get-tuple-element.47), channel_id=1, source_target_pairs={{0,1},{1,2},{2,3},{3,4},{4,5},{5,6},{6,7},{8,9},{9,10},{10,11},{11... | collective-permute-start | bytes 122888 | tf_op jit(solution)/shard_map/ppermute | solution.py:16
  12.0 20.7 %collective-permute-start.3 = (f32[2,5,1024]{2,1,0:T(8,128)S(1)}, f32[2,5,1024]{2,1,0:T(8,128)S(1)}, u32[]{:S(2)}, u32[]{:S(2)}) collective-permute-start(f32[2,5,1024]{2,1,0:T(8,128)S(1)} %get-tuple-element.48), channel_id=1, source_target_pairs={{1,0},{2,1},{3,2},{4,3},{5,4},{6,5},{7,6},{9,8},{10,9},{11,10},{12... | collective-permute-start | bytes 122888 | tf_op jit(solution)/shard_map/ppermute | solution.py:17
  19.3 13.3 %copy-start.4 = (f32[8,1024]{1,0:T(8,128)S(1)}, f32[8,1024]{1,0:T(8,128)}, u32[]{:S(2)}) copy-start(f32[8,1024]{1,0:T(8,128)} %param.9) | copy-start | bytes 98308
  43.7 26.5 %collective-permute-start = (f32[3,45,1,1024]{3,2,1,0:T(1,128)S(1)}, f32[3,45,1,1024]{3,2,1,0:T(1,128)S(1)}, u32[]{:S(2)}, u32[]{:S(2)}) collective-permute-start(f32[3,45,1,1024]{3,2,1,0:T(1,128)S(1)} %get-tuple-element.78), channel_id=1, source_target_pairs={{1,0},{2,1},{3,2},{4,3},{5,4},{6,5},{7,6},{9,8},{10,9},{11,10},{12... | collective-permute-start | bytes 1658888 | tf_op jit(solution)/shard_map/while/body/eval_jaxpr/ppermute | solution.py:17
  45.8 25.1 %collective-permute-start.1 = (f32[3,45,1,1024]{3,2,1,0:T(1,128)S(1)}, f32[3,45,1,1024]{3,2,1,0:T(1,128)S(1)}, u32[]{:S(2)}, u32[]{:S(2)}) collective-permute-start(f32[3,45,1,1024]{3,2,1,0:T(1,128)S(1)} %get-tuple-element.79), channel_id=1, source_target_pairs={{0,1},{1,2},{2,3},{3,4},{4,5},{5,6},{6,7},{8,9},{9,10},{10,11},{11... | collective-permute-start | bytes 1658888 | tf_op jit(solution)/shard_map/while/body/eval_jaxpr/ppermute | solution.py:16
  117.9 27.9 %collective-permute-start = (f32[3,45,1,1024]{3,2,1,0:T(1,128)S(1)}, f32[3,45,1,1024]{3,2,1,0:T(1,128)S(1)}, u32[]{:S(2)}, u32[]{:S(2)}) collective-permute-start(f32[3,45,1,1024]{3,2,1,0:T(1,128)S(1)} %get-tuple-element.78), channel_id=1, source_target_pairs={{1,0},{2,1},{3,2},{4,3},{5,4},{6,5},{7,6},{9,8},{10,9},{11,10},{12... | collective-permute-start | bytes 1658888 | tf_op jit(solution)/shard_map/while/body/eval_jaxpr/ppermute | solution.py:17
  121.9 25.1 %collective-permute-start.1 = (f32[3,45,1,1024]{3,2,1,0:T(1,128)S(1)}, f32[3,45,1,1024]{3,2,1,0:T(1,128)S(1)}, u32[]{:S(2)}, u32[]{:S(2)}) collective-permute-start(f32[3,45,1,1024]{3,2,1,0:T(1,128)S(1)} %get-tuple-element.79), channel_id=1, source_target_pairs={{0,1},{1,2},{2,3},{3,4},{4,5},{5,6},{6,7},{8,9},{9,10},{10,11},{11... | collective-permute-start | bytes 1658888 | tf_op jit(solution)/shard_map/while/body/eval_jaxpr/ppermute | solution.py:16
  193.9 28.4 %collective-permute-start = (f32[3,45,1,1024]{3,2,1,0:T(1,128)S(1)}, f32[3,45,1,1024]{3,2,1,0:T(1,128)S(1)}, u32[]{:S(2)}, u32[]{:S(2)}) collective-permute-start(f32[3,45,1,1024]{3,2,1,0:T(1,128)S(1)} %get-tuple-element.78), channel_id=1, source_target_pairs={{1,0},{2,1},{3,2},{4,3},{5,4},{6,5},{7,6},{9,8},{10,9},{11,10},{12... | collective-permute-start | bytes 1658888 | tf_op jit(solution)/shard_map/while/body/eval_jaxpr/ppermute | solution.py:17
  198.0 25.1 %collective-permute-start.1 = (f32[3,45,1,1024]{3,2,1,0:T(1,128)S(1)}, f32[3,45,1,1024]{3,2,1,0:T(1,128)S(1)}, u32[]{:S(2)}, u32[]{:S(2)}) collective-permute-start(f32[3,45,1,1024]{3,2,1,0:T(1,128)S(1)} %get-tuple-element.79), channel_id=1, source_target_pairs={{0,1},{1,2},{2,3},{3,4},{4,5},{5,6},{6,7},{8,9},{9,10},{10,11},{11... | collective-permute-start | bytes 1658888 | tf_op jit(solution)/shard_map/while/body/eval_jaxpr/ppermute | solution.py:16
  270.0 28.4 %collective-permute-start = (f32[3,45,1,1024]{3,2,1,0:T(1,128)S(1)}, f32[3,45,1,1024]{3,2,1,0:T(1,128)S(1)}, u32[]{:S(2)}, u32[]{:S(2)}) collective-permute-start(f32[3,45,1,1024]{3,2,1,0:T(1,128)S(1)} %get-tuple-element.78), channel_id=1, source_target_pairs={{1,0},{2,1},{3,2},{4,3},{5,4},{6,5},{7,6},{9,8},{10,9},{11,10},{12... | collective-permute-start | bytes 1658888 | tf_op jit(solution)/shard_map/while/body/eval_jaxpr/ppermute | solution.py:17
  274.0 25.1 %collective-permute-start.1 = (f32[3,45,1,1024]{3,2,1,0:T(1,128)S(1)}, f32[3,45,1,1024]{3,2,1,0:T(1,128)S(1)}, u32[]{:S(2)}, u32[]{:S(2)}) collective-permute-start(f32[3,45,1,1024]{3,2,1,0:T(1,128)S(1)} %get-tuple-element.79), channel_id=1, source_target_pairs={{0,1},{1,2},{2,3},{3,4},{4,5},{5,6},{6,7},{8,9},{9,10},{10,11},{11... | collective-permute-start | bytes 1658888 | tf_op jit(solution)/shard_map/while/body/eval_jaxpr/ppermute | solution.py:16
  346.1 28.4 %collective-permute-start = (f32[3,45,1,1024]{3,2,1,0:T(1,128)S(1)}, f32[3,45,1,1024]{3,2,1,0:T(1,128)S(1)}, u32[]{:S(2)}, u32[]{:S(2)}) collective-permute-start(f32[3,45,1,1024]{3,2,1,0:T(1,128)S(1)} %get-tuple-element.78), channel_id=1, source_target_pairs={{1,0},{2,1},{3,2},{4,3},{5,4},{6,5},{7,6},{9,8},{10,9},{11,10},{12... | collective-permute-start | bytes 1658888 | tf_op jit(solution)/shard_map/while/body/eval_jaxpr/ppermute | solution.py:17
  350.1 25.1 %collective-permute-start.1 = (f32[3,45,1,1024]{3,2,1,0:T(1,128)S(1)}, f32[3,45,1,1024]{3,2,1,0:T(1,128)S(1)}, u32[]{:S(2)}, u32[]{:S(2)}) collective-permute-start(f32[3,45,1,1024]{3,2,1,0:T(1,128)S(1)} %get-tuple-element.79), channel_id=1, source_target_pairs={{0,1},{1,2},{2,3},{3,4},{4,5},{5,6},{6,7},{8,9},{9,10},{10,11},{11... | collective-permute-start | bytes 1658888 | tf_op jit(solution)/shard_map/while/body/eval_jaxpr/ppermute | solution.py:16
  422.1 28.4 %collective-permute-start = (f32[3,45,1,1024]{3,2,1,0:T(1,128)S(1)}, f32[3,45,1,1024]{3,2,1,0:T(1,128)S(1)}, u32[]{:S(2)}, u32[]{:S(2)}) collective-permute-start(f32[3,45,1,1024]{3,2,1,0:T(1,128)S(1)} %get-tuple-element.78), channel_id=1, source_target_pairs={{1,0},{2,1},{3,2},{4,3},{5,4},{6,5},{7,6},{9,8},{10,9},{11,10},{12... | collective-permute-start | bytes 1658888 | tf_op jit(solution)/shard_map/while/body/eval_jaxpr/ppermute | solution.py:17
  426.1 25.1 %collective-permute-start.1 = (f32[3,45,1,1024]{3,2,1,0:T(1,128)S(1)}, f32[3,45,1,1024]{3,2,1,0:T(1,128)S(1)}, u32[]{:S(2)}, u32[]{:S(2)}) collective-permute-start(f32[3,45,1,1024]{3,2,1,0:T(1,128)S(1)} %get-tuple-element.79), channel_id=1, source_target_pairs={{0,1},{1,2},{2,3},{3,4},{4,5},{5,6},{6,7},{8,9},{9,10},{10,11},{11... | collective-permute-start | bytes 1658888 | tf_op jit(solution)/shard_map/while/body/eval_jaxpr/ppermute | solution.py:16
  498.2 28.4 %collective-permute-start = (f32[3,45,1,1024]{3,2,1,0:T(1,128)S(1)}, f32[3,45,1,1024]{3,2,1,0:T(1,128)S(1)}, u32[]{:S(2)}, u32[]{:S(2)}) collective-permute-start(f32[3,45,1,1024]{3,2,1,0:T(1,128)S(1)} %get-tuple-element.78), channel_id=1, source_target_pairs={{1,0},{2,1},{3,2},{4,3},{5,4},{6,5},{7,6},{9,8},{10,9},{11,10},{12... | collective-permute-start | bytes 1658888 | tf_op jit(solution)/shard_map/while/body/eval_jaxpr/ppermute | solution.py:17
  502.2 25.1 %collective-permute-start.1 = (f32[3,45,1,1024]{3,2,1,0:T(1,128)S(1)}, f32[3,45,1,1024]{3,2,1,0:T(1,128)S(1)}, u32[]{:S(2)}, u32[]{:S(2)}) collective-permute-start(f32[3,45,1,1024]{3,2,1,0:T(1,128)S(1)} %get-tuple-element.79), channel_id=1, source_target_pairs={{0,1},{1,2},{2,3},{3,4},{4,5},{5,6},{6,7},{8,9},{9,10},{10,11},{11... | collective-permute-start | bytes 1658888 | tf_op jit(solution)/shard_map/while/body/eval_jaxpr/ppermute | solution.py:16
  574.2 28.4 %collective-permute-start = (f32[3,45,1,1024]{3,2,1,0:T(1,128)S(1)}, f32[3,45,1,1024]{3,2,1,0:T(1,128)S(1)}, u32[]{:S(2)}, u32[]{:S(2)}) collective-permute-start(f32[3,45,1,1024]{3,2,1,0:T(1,128)S(1)} %get-tuple-element.78), channel_id=1, source_target_pairs={{1,0},{2,1},{3,2},{4,3},{5,4},{6,5},{7,6},{9,8},{10,9},{11,10},{12... | collective-permute-start | bytes 1658888 | tf_op jit(solution)/shard_map/while/body/eval_jaxpr/ppermute | solution.py:17
  578.2 25.1 %collective-permute-start.1 = (f32[3,45,1,1024]{3,2,1,0:T(1,128)S(1)}, f32[3,45,1,1024]{3,2,1,0:T(1,128)S(1)}, u32[]{:S(2)}, u32[]{:S(2)}) collective-permute-start(f32[3,45,1,1024]{3,2,1,0:T(1,128)S(1)} %get-tuple-element.79), channel_id=1, source_target_pairs={{0,1},{1,2},{2,3},{3,4},{4,5},{5,6},{6,7},{8,9},{9,10},{10,11},{11... | collective-permute-start | bytes 1658888 | tf_op jit(solution)/shard_map/while/body/eval_jaxpr/ppermute | solution.py:16
  650.3 28.4 %collective-permute-start = (f32[3,45,1,1024]{3,2,1,0:T(1,128)S(1)}, f32[3,45,1,1024]{3,2,1,0:T(1,128)S(1)}, u32[]{:S(2)}, u32[]{:S(2)}) collective-permute-start(f32[3,45,1,1024]{3,2,1,0:T(1,128)S(1)} %get-tuple-element.78), channel_id=1, source_target_pairs={{1,0},{2,1},{3,2},{4,3},{5,4},{6,5},{7,6},{9,8},{10,9},{11,10},{12... | collective-permute-start | bytes 1658888 | tf_op jit(solution)/shard_map/while/body/eval_jaxpr/ppermute | solution.py:17
  654.3 25.1 %collective-permute-start.1 = (f32[3,45,1,1024]{3,2,1,0:T(1,128)S(1)}, f32[3,45,1,1024]{3,2,1,0:T(1,128)S(1)}, u32[]{:S(2)}, u32[]{:S(2)}) collective-permute-start(f32[3,45,1,1024]{3,2,1,0:T(1,128)S(1)} %get-tuple-element.79), channel_id=1, source_target_pairs={{0,1},{1,2},{2,3},{3,4},{4,5},{5,6},{6,7},{8,9},{9,10},{10,11},{11... | collective-permute-start | bytes 1658888 | tf_op jit(solution)/shard_map/while/body/eval_jaxpr/ppermute | solution.py:16
  726.4 28.4 %collective-permute-start = (f32[3,45,1,1024]{3,2,1,0:T(1,128)S(1)}, f32[3,45,1,1024]{3,2,1,0:T(1,128)S(1)}, u32[]{:S(2)}, u32[]{:S(2)}) collective-permute-start(f32[3,45,1,1024]{3,2,1,0:T(1,128)S(1)} %get-tuple-element.78), channel_id=1, source_target_pairs={{1,0},{2,1},{3,2},{4,3},{5,4},{6,5},{7,6},{9,8},{10,9},{11,10},{12... | collective-permute-start | bytes 1658888 | tf_op jit(solution)/shard_map/while/body/eval_jaxpr/ppermute | solution.py:17
  730.4 25.1 %collective-permute-start.1 = (f32[3,45,1,1024]{3,2,1,0:T(1,128)S(1)}, f32[3,45,1,1024]{3,2,1,0:T(1,128)S(1)}, u32[]{:S(2)}, u32[]{:S(2)}) collective-permute-start(f32[3,45,1,1024]{3,2,1,0:T(1,128)S(1)} %get-tuple-element.79), channel_id=1, source_target_pairs={{0,1},{1,2},{2,3},{3,4},{4,5},{5,6},{6,7},{8,9},{9,10},{10,11},{11... | collective-permute-start | bytes 1658888 | tf_op jit(solution)/shard_map/while/body/eval_jaxpr/ppermute | solution.py:16
  (51 other events, 316.0 us)
Sparse Core Ops, SparseCore 0:
  842.4 23.1 reduce-scatter.1
where the time goes:
time: 887 us; the launch traced here: 883 us
  other arithmetic  300 us (34%)
  waiting for transfers between devices  253 us (29%)
  local copies, waits for them, and re-layouts  233 us (26%)
  starting transfers between devices  65.8 us (7%)
  matrix products  17.6 us (2%)
  between operations  14.1 us (2%)
    ppermute x11, waiting for transfers between devices, extended_2(): after = lax.ppermute(first, axis, down)  222 us
    add x10, other arithmetic, smooth(): return current + east_side + north_side  171 us
    mul x10, other arithmetic, smooth(): east_flux = east_weight * (jnp.roll(current, -1, 3) - current)  82.7 us
    slice x20, local copies, waits for them, and re-layouts, smooth(): east_flux = east_weight * (jnp.roll(current, -1, 3) - current)  62 us
    while x100, local copies, waits for them, and re-layouts  60.5 us
    slice x10, local copies, waits for them, and re-layouts, extended_2(): first = lax.slice_in_dim(value, 0, width, axis=dim)  48.2 us
    ppermute x11, starting transfers between devices, extended_2(): after = lax.ppermute(first, axis, down)  41.2 us
    concatenate x10, other arithmetic, extended_2(): value = jnp.concatenate([before, value, after], axis=dim)  34.5 us
  transfers between devices with their start and end apart: 23, of which 21 were waited for; matrix products, arithmetic and copies ran while one was open for 2% of the time, Pallas kernels for 0%

commit v1 on v0

v1 whole, which is shorter than its diff:
```python
import jax
import jax.numpy as jnp
from jax import lax
from jax.experimental import pallas as pl
from jax.experimental.pallas import tpu as pltpu
from jax.sharding import PartitionSpec as P

ITERS = 10
TURN_COST = 20
GATHER_COST = 20
FILTER_COST = 1
PROJECT_COST = 20
GROUP = 8
LANES = 128
PLANES = 4
F32 = jnp.float32
BF16 = jnp.bfloat16


def whole(space=pltpu.VMEM):
    return pl.BlockSpec(memory_space=space)


def call(body, landed=(), **kw):
    shapes = tuple(pltpu.HBM(a.shape, a.dtype) for a in kw.pop("out_shape"))
    inner = pl.pallas_call(body, out_shape=shapes, **kw)

    def run(*args):
        pinned = []
        for i, (arg, spec) in enumerate(zip(args, kw["in_specs"])):
            if spec.memory_space != pltpu.SMEM:
                space = pltpu.VMEM if i in landed else pltpu.HBM
                arg = pltpu.with_memory_space_constraint(arg, space)
            pinned.append(arg)
        return inner(*pinned)

    return run


def params(mib):
    return pltpu.CompilerParams(vmem_limit_bytes=mib * 1024 * 1024)


def cost(us):
    return pl.CostEstimate(flops=0, transcendentals=0, bytes_accessed=us * 3_690_000)


def spread_fill(spread_ref, unspread_ref):
    cols = spread_ref.shape[0]
    tiles = cols // LANES
    for first in range(0, cols, LANES):
        here = first + lax.broadcasted_iota(jnp.int32, (LANES, cols), 0)
        there = lax.broadcasted_iota(jnp.int32, (LANES, cols), 1)
        rows = pl.ds(first, LANES)
        to_spot = here == (there % LANES) * tiles + there // LANES
        to_col = there == (here % LANES) * tiles + here // LANES
        spread_ref[rows, :] = jnp.where(to_spot, 1.0, 0.0).astype(BF16)
        unspread_ref[rows, :] = jnp.where(to_col, 1.0, 0.0).astype(BF16)


def turn_piece(piece, spread_ref, turn_ref, put, put_statics=None):
    count, rows, cols = piece.shape
    flat = piece.astype(F32).reshape(count * rows, cols).astype(BF16)
    moved = jnp.dot(flat, spread_ref[...], preferred_element_type=F32)
    fields = count // GROUP
    for j in range(cols // LANES):
        turn_ref[j, pl.ds(0, count * rows), :] = moved[:, j * LANES : (j + 1) * LANES]
    for j in range(cols // LANES):
        lanes = pl.ds(j * LANES, LANES)
        for r in range(rows):
            for f in range(fields):
                value = turn_ref[j, pl.ds(f * GROUP * rows + r, GROUP, stride=rows), :]
                put(r, f, fields, lanes, value.astype(BF16))
            if put_statics is not None:
                first = fields * GROUP * rows + r
                put_statics(r, lanes, turn_ref[j, pl.ds(first, PLANES, stride=rows), :])


def turn_body(base_ref, fields_ref, planes_ref, spread_ref, unspread_ref, statics_ref, *refs):
    buf_ref, turn_ref, sems = refs[-3:]
    outs = refs[:-3]
    _, fields, _, rows, cols = buf_ref.shape
    copies = [
        pltpu.make_async_copy(
            fields_ref.at[:, pl.ds(base_ref[n], GROUP)], buf_ref.at[n], sems.at[n]
        )
        for n in range(len(outs))
    ]
    for copy in copies:
        copy.start()
    spread_fill(spread_ref, unspread_ref)
    for n, out in enumerate(outs):
        copies[n].wait()

        def put(r, f, count, lanes, value):
            out[r * count + f, :, lanes] = value

        def put_statics(r, lanes, value):
            at = r * PLANES
            statics_ref[at // GROUP, pl.ds(at % GROUP, PLANES), lanes] = value

        piece = buf_ref[n].reshape(fields * GROUP, rows, cols)
        if n == 0:
            piece = jnp.concatenate([piece, planes_ref[...]], axis=0)
        turn_piece(piece, spread_ref, turn_ref, put, put_statics if n == 0 else None)


def turn(bases, fields, planes):
    count, _, rows, cols = fields.shape
    out = jax.ShapeDtypeStruct((rows * count, GROUP, cols), BF16)
    square = jax.ShapeDtypeStruct((cols, cols), BF16)
    many = len(bases)
    return call(
        turn_body,
        out_shape=(square, square, jax.ShapeDtypeStruct((rows * PLANES // GROUP, GROUP, cols), F32))
        + (out,) * many,
        in_specs=[whole(pltpu.SMEM), whole(pl.ANY), whole()],
        out_specs=(whole(),) * (3 + many),
        scratch_shapes=[
            pltpu.VMEM((many, count, GROUP, rows, cols), BF16),
            pltpu.VMEM((cols // LANES, (count * GROUP + PLANES) * rows, LANES), F32),
            pltpu.SemaphoreType.DMA((many,)),
        ],
        compiler_params=params(16),
        cost_estimate=cost(TURN_COST),
        name="turn",
    )(jnp.stack(bases), fields, planes)


def gather_body(where_ref, own_ref, part_ref, spread_ref, *refs):
    refs = list(refs)
    own_statics_ref = refs.pop(0) if len(refs) > 4 else None
    pair_ref, first_ref, second_ref, turn_ref = refs[:4]
    statics_ref = refs[4] if own_statics_ref is not None else None
    rows = part_ref.shape[1]
    fields = own_ref.shape[0] // rows
    side, odd = (where_ref[0], where_ref[1])
    own_start = side * rows
    part_start = rows - own_start
    for r in range(rows * fields):
        pair_ref[own_start * fields + r] = own_ref[r]

    def put(r, f, count, lanes, value):
        pair_ref[(part_start + r) * count + f, :, lanes] = value

    put_statics = None
    if statics_ref is not None:
        tiles = rows * PLANES // GROUP
        statics_ref[pl.ds(side * tiles, tiles)] = own_statics_ref[...]

        def put_statics(r, lanes, value):
            at = r * PLANES
            base = (1 - side) * tiles + at // GROUP
            statics_ref[base, pl.ds(at % GROUP, PLANES), lanes] = value

    turn_piece(part_ref[...], spread_ref, turn_ref, put, put_statics)
    tail = 2 * rows - ITERS
    for dst, pick in ((first_ref, 1 - odd), (second_ref, odd)):
        for r in range(ITERS * fields):
            dst[r] = pair_ref[pick * tail * fields + r]
        if statics_ref is not None:
            count = ITERS * PLANES // GROUP
            value = statics_ref[pl.ds(pick * (tail * PLANES // GROUP), count)]
            dst[pl.ds(ITERS * fields, count)] = value.astype(BF16)
    if statics_ref is not None:
        pair_ref[pl.ds(2 * rows * fields, statics_ref.shape[0])] = statics_ref[...].astype(BF16)


def gather_rows(where, own, part, spread, statics=None):
    count, rows, cols = part.shape
    fields = own.shape[0] // rows
    extra = 0 if statics is None else PLANES

    def out(n):
        return jax.ShapeDtypeStruct((n * fields + n * extra // GROUP, GROUP, cols), BF16)

    scratch = [pltpu.VMEM((cols // LANES, count * rows, LANES), F32)]
    if statics is not None:
        scratch.append(pltpu.VMEM((2 * rows * PLANES // GROUP, GROUP, cols), F32))
    args = (where, own, part, spread) + (() if statics is None else (statics,))
    return call(
        gather_body,
        landed=(2,),
        out_shape=(out(2 * rows), out(ITERS), out(ITERS)),
        in_specs=[whole(pltpu.SMEM)] + [whole()] * (len(args) - 1),
        out_specs=(whole(),) * 3,
        scratch_shapes=scratch,
        compiler_params=params(16),
        cost_estimate=cost(GATHER_COST),
        name="gather_rows",
    )(*args)


def make_faces(face_ref, planes_ref, spare_ref):
    _, tiles, total, _ = face_ref.shape
    spare_ref[...] = jnp.zeros(spare_ref.shape, F32)

    def plane(j, p):
        return planes_ref[j, pl.ds(p, total, stride=PLANES), :]

    for j in range(tiles):
        spare_ref[0, j, pl.ds(0, total), :] = plane(j, 0) + plane(j, 1) + plane(j, 2)
        spare_ref[1, j, pl.ds(0, total), :] = plane(j, 3)
    lane = lax.broadcasted_iota(jnp.int32, (total, LANES), 1)
    for j in range(tiles):
        here, east, north = ([], [], [])
        for i in range(2):
            here.append(spare_ref[i, j, pl.ds(0, total), :])
            if j + 1 < tiles:
                east.append(spare_ref[i, j + 1, pl.ds(0, total), :])
            else:
                east.append(pltpu.roll(spare_ref[i, 0], LANES - 1, 1)[:total])
            north.append(spare_ref[i, j, pl.ds(1, total), :])
        wet_east = jnp.minimum(here[1], east[1])
        if j + 1 == tiles:
            wet_east = jnp.where(lane == LANES - 1, 0.0, wet_east)
        face_ref[0, j] = 0.5 * (here[0] + east[0])
        face_ref[1, j] = wet_east
        face_ref[2, j] = 0.5 * (here[0] + north[0])
        face_ref[3, j] = jnp.minimum(here[1], north[1])


def filter_body(leads, scal_ref, pair_ref, first_ref, second_ref, back_ref, *refs):
    face_ref, mine_ref, send_ref = refs[:3]
    cur_ref, east_ref, west_ref, north_ref, turn_ref = refs[3:8]
    fields, total, tiles, _, _ = cur_ref.shape
    cols = tiles * LANES
    pair = total - 2 * ITERS
    rows = pair // 2
    side = scal_ref[0]
    level = (scal_ref[2] + lax.broadcasted_iota(jnp.int32, (GROUP, LANES), 0)).astype(F32)

    def fill(src, dst_row, count):
        for r in range(count):
            for f in range(fields):
                for j in range(tiles):
                    value = src[r * fields + f, :, pl.ds(j * LANES, LANES)]
                    cur_ref[f, dst_row + r, j] = value.astype(F32)
        if leads:
            planes_ref = refs[8]
            block = count * PLANES
            for j in range(tiles):
                value = src[pl.ds(count * fields, block // GROUP), :, pl.ds(j * LANES, LANES)]
                planes_ref[j, pl.ds(dst_row * PLANES, block), :] = value.astype(F32).reshape(
                    block, LANES
                )

    @pl.when(scal_ref[1] == 0)
    def _():
        fill(second_ref, 0, ITERS)
        fill(first_ref, ITERS + pair, ITERS)

    @pl.when(scal_ref[1] == 1)
    def _():
        fill(first_ref, 0, ITERS)
        fill(second_ref, ITERS + pair, ITERS)

    fill(pair_ref, ITERS, pair)
    if leads:
        make_faces(face_ref, refs[8], refs[9])

    def weights(r, _):
        for j in range(tiles):

            def spread(i):
                return jnp.broadcast_to(face_ref[i, j, pl.ds(r, 1), :], (GROUP, LANES))

            east = jnp.where(level < spread(1), spread(0), 0.0)
            east_ref[r, j] = east
            north_ref[r, j] = jnp.where(level < spread(3), spread(2), 0.0)
        west_ref[r] = pltpu.roll(east, 1, 1)
        return 0

    lax.fori_loop(0, total, weights, 0, unroll=4)

    def one_field(f, _):
        for step in range(1, ITERS + 1):
            here = [cur_ref[f, step, j] for j in range(tiles)]
            south = [
                north_ref[step - 1, j] * (here[j] - cur_ref[f, step - 1, j]) for j in range(tiles)
            ]
            first = pltpu.roll(here[0], LANES - 1, 1)
            last = pltpu.roll(here[-1], 1, 1)
            for r in range(step, total - step):
                ahead = [cur_ref[f, r + 1, j] for j in range(tiles)]
                flux = west_ref[r] * (here[0] - last)
                for j in range(tiles):
                    beyond = here[j + 1] if j + 1 < tiles else first
                    east = east_ref[r, j] * (beyond - here[j])
                    north = north_ref[r, j] * (ahead[j] - here[j])
                    cur_ref[f, r, j] = here[j] + (east - flux) + (north - south[j])
                    flux = east
                    south[j] = north
                first = pltpu.roll(ahead[0], LANES - 1, 1)
                last = pltpu.roll(ahead[-1], 1, 1)
                here = ahead
        return 0

    lax.fori_loop(0, fields, one_field, 0)

    def emit(dst, start):
        for f in range(fields):
            for r in range(rows):
                for j in range(tiles):
                    spots = pl.ds(f * GROUP * rows + r, GROUP, stride=rows)
                    turn_ref[j, spots, :] = cur_ref[f, start + r, j]
        flat = jnp.concatenate([turn_ref[j].astype(BF16) for j in range(tiles)], axis=1)
        moved = jnp.dot(flat, back_ref[...], preferred_element_type=F32)
        dst[...] = moved.reshape(fields, GROUP, rows, cols).astype(BF16)

    emit(send_ref, ITERS + rows * (1 - side))
    emit(mine_ref, ITERS + rows * side)


def filter_rows(scalars, pair, first, second, unspread, faces, fields, rows):
    cols = pair.shape[2]
    total = 2 * rows + 2 * ITERS
    tiles = cols // LANES
    leads = faces is None
    out = jax.ShapeDtypeStruct((fields, GROUP, rows, cols), BF16)
    face = jax.ShapeDtypeStruct((4, tiles, total, LANES), F32)
    scratch = [
        pltpu.VMEM((fields, total, tiles, GROUP, LANES), F32),
        pltpu.VMEM((total, tiles, GROUP, LANES), F32),
        pltpu.VMEM((total, GROUP, LANES), F32),
        pltpu.VMEM((total, tiles, GROUP, LANES), F32),
        pltpu.VMEM((tiles, fields * GROUP * rows, LANES), F32),
    ]
    if leads:
        spare = -(-(total + 1) // GROUP) * GROUP
        scratch += [
            pltpu.VMEM((tiles, total * PLANES, LANES), F32),
            pltpu.VMEM((2, tiles, spare, LANES), F32),
        ]

    def body(*refs):
        filter_body(leads, *refs)

    return call(
        body,
        landed=(2, 3),
        out_shape=((face,) if leads else ()) + (out, out),
        in_specs=[whole(pltpu.SMEM)]
        + [whole()] * 4
        + ([] if leads else [whole()]),
        out_specs=(whole(),) * (3 if leads else 2),
        scratch_shapes=scratch,
        compiler_params=params(24),
        cost_estimate=cost(FILTER_COST),
        name="filter_rows",
    )(scalars, pair, first, second, unspread, *(() if leads else (faces,)))


def project_body(takes, halves, has_start, base_ref, *refs):
    count = len(takes)
    refs = list(refs)
    chunk_refs = refs[:count]
    refs = refs[count:]
    modes_ref = refs.pop(0)
    start_ref = None
    if has_start:
        start_ref = refs.pop(0)
        refs.pop(0)
    out_ref = refs.pop(0)
    keep_ref = give_ref = amp_ref = None
    if halves > 1:
        keep_ref, give_ref = (refs.pop(0), refs.pop(0))
    else:
        amp_ref = refs.pop(0)
    mode_bufs = refs[:count]
    out_sems, mode_sems = refs[count:]
    fields, _, rows, cols = chunk_refs[0].shape
    modes = modes_ref.shape[0]
    fetches = [
        pltpu.make_async_copy(
            modes_ref.at[:, pl.ds(base_ref[n, 0], takes[n])], mode_bufs[n], mode_sems.at[n]
        )
        for n in range(count)
    ]
    copies = [
        pltpu.make_async_copy(
            chunk_refs[n].at[:, pl.ds(base_ref[n, 1], takes[n])],
            out_ref.at[:, pl.ds(base_ref[n, 0], takes[n])],
            out_sems.at[n],
        )
        for n in range(count)
    ]
    for fetch in fetches:
        fetch.start()
    for copy in copies:
        copy.start()
    for n in range(count):
        fetches[n].wait()

        def one_tile(tile, dst, dst_tile, _):
            lanes = pl.ds(pl.multiple_of(tile * LANES, LANES), LANES)
            into = pl.ds(pl.multiple_of(dst_tile * LANES, LANES), LANES)
            sums = []
            for f in range(fields):
                for k in range(modes):
                    if n > 0:
                        sums.append(amp_ref[f, k, :, lanes])
                    elif has_start:
                        sums.append(start_ref[f, k, :, lanes])
                    else:
                        sums.append(jnp.zeros((rows, LANES), F32))
            for i in range(takes[n]):
                values = [
                    chunk_refs[n][f, base_ref[n, 1] + i, :, lanes].astype(F32)
                    for f in range(fields)
                ]
                for k in range(modes):
                    mode = mode_bufs[n][k, i, :, lanes].astype(F32)
                    for f in range(fields):
                        sums[f * modes + k] = sums[f * modes + k] + mode * values[f]
            for f in range(fields):
                for k in range(modes):
                    dst[f, k, :, into] = sums[f * modes + k]
            return 0

        tiles = cols // LANES
        if halves == 1:
            lax.fori_loop(0, tiles, lambda i, z: one_tile(i, amp_ref, i, z), 0)
        else:
            width = tiles // halves
            mine = base_ref[n, 2] * width
            rest = (1 - base_ref[n, 2]) * width
            lax.fori_loop(0, width, lambda i, z: one_tile(rest + i, give_ref, i, z), 0)
            lax.fori_loop(0, width, lambda i, z: one_tile(mine + i, keep_ref, i, z), 0)
    for copy in copies:
        copy.wait()


def project(bases, chunks, takes, vertical_modes, levels, halves, carried=()):
    count = len(chunks)
    fields, _, rows, cols = chunks[0].shape
    modes = vertical_modes.shape[0]

    def body(*refs):
        project_body(takes, halves, bool(carried), *refs)

    amplitude = jax.ShapeDtypeStruct((fields, modes, rows, cols // halves), F32)

    return call(
        body,
        landed=(1,) if carried else (),
        out_shape=(jax.ShapeDtypeStruct((fields, levels, rows, cols), BF16),)
        + (amplitude,) * halves,
        in_specs=[whole(pltpu.SMEM)]
        + [whole()] * count
        + [whole(pl.ANY)]
        + ([whole(), whole(pl.ANY)] if carried else []),
        out_specs=(whole(pl.ANY),) + (whole(),) * halves,
        input_output_aliases={count + 3: 0} if carried else {},
        scratch_shapes=[pltpu.VMEM((modes, take, rows, cols), BF16) for take in takes]
        + [pltpu.SemaphoreType.DMA((count,))] * 2,
        compiler_params=params(24),
        cost_estimate=cost(PROJECT_COST),
        name="project",
    )(bases, *chunks, vertical_modes, *carried)


def flux_body(keep_ref, other_ref, out_ref):
    total = keep_ref[...] + other_ref[...]
    out_ref[0] = total[0] * total[2]
    out_ref[1] = total[1] * total[2]
    out_ref[2] = 0.5 * (total[0] * total[0] + total[1] * total[1])


def statics_planes(diffusivity, depth):
    high = lax.reduce_precision(diffusivity, 8, 7)
    middle = lax.reduce_precision(diffusivity - high, 8, 7)
    low = diffusivity - high - middle
    return jnp.stack([high, middle, low, depth]).astype(BF16)


def per_device(fields, vertical_modes, diffusivity, land_mask, wet_levels):
    count, levels, rows, cols = fields.shape
    size = lax.axis_size("row")
    row = lax.axis_index("row")
    lev = lax.axis_index("lev")
    side = row % 2
    pairs = [(i, i ^ 1) for i in range(size)]
    odd = (row // 2) % 2
    near = [(i, i ^ 2) for i in range(size)]
    far = [(i, ((i + 2) ^ 2) - 2) for i in range(2, size - 2)]
    chunks = -(-(-(-levels // 2)) // GROUP)

    def base(c, which):
        return jnp.where(which == 0, GROUP * c, levels - GROUP * (c + 1)).astype(jnp.int32)

    theirs = [base(c, 1 - side) for c in range(chunks)]
    ours = [base(c, side) for c in range(chunks)]
    depth = (land_mask * wet_levels).astype(F32)
    planes = statics_planes(diffusivity, depth)
    parts = []
    for c, b in enumerate(theirs):
        piece = lax.dynamic_slice_in_dim(fields, b, GROUP, 1)
        piece = piece.reshape(count * GROUP, rows, cols)
        if c == 0:
            piece = jnp.concatenate([piece, planes], axis=0)
        parts.append(lax.ppermute(piece, "row", pairs))
    spread, unspread, statics, *owns = turn(ours, fields, planes)

    where = jnp.stack([side, odd])
    mine, returned, edges = ([], [], [])
    faces = None
    for c in range(chunks):
        part = parts[c]
        if c > 0:
            part, *_ = lax.optimization_barrier((part, edges[-1], mine[: c - 1]))
        pair, first, second = gather_rows(
            where, owns[c], part, spread, statics if c == 0 else None
        )
        edges.append(first)
        first = lax.ppermute(first, "row", near)
        second = lax.ppermute(second, "row", far)
        if c > 0:
            first, *_ = lax.optimization_barrier((first, mine[-1], returned[: c - 1]))
        scalars = jnp.stack([side, odd, lev * levels + ours[c]])
        *lead, kept, sent = filter_rows(
            scalars, pair, first, second, unspread, faces, count, rows
        )
        if c == 0:
            faces = lead[0]
        mine.append(kept)
        returned.append(lax.ppermute(sent, "row", pairs))

    cut = levels - (2 * chunks - 1) * GROUP
    first = jnp.where(side == 0, GROUP - cut, 0).astype(jnp.int32)
    zero = jnp.zeros((), jnp.int32)
    bases = [jnp.stack([b, zero]) for b in ours + theirs[:-1]]
    filtered, amplitude = project(
        jnp.stack(bases),
        mine + returned[:-1],
        [GROUP] * (2 * chunks - 1),
        vertical_modes,
        levels,
        1,
    )
    filtered, keep, give = project(
        jnp.stack([theirs[-1] + first, first, lev])[None],
        returned[-1:],
        [cut],
        vertical_modes,
        levels,
        lax.axis_size("lev"),
        (amplitude, filtered),
    )
    other = lax.ppermute(give, "lev", [(0, 1), (1, 0)])
    modal_flux = pl.pallas_call(
        flux_body, out_shape=jax.ShapeDtypeStruct(keep.shape, F32), name="flux"
    )(keep, other)
    return (filtered, modal_flux)


def solution(mesh):
    placed = (
        P("group", "lev", "row", None),
        P(None, "lev", "row", None),
        P("row", None),
        P("row", None),
        P("row", None),
    )
    return jax.shard_map(
        per_device,
        mesh=mesh,
        in_specs=placed,
        out_specs=(P("group", "lev", "row", None), P("group", None, "row", "lev")),
        check_vma=False,
    )
```

time: 887 us -> 106 us (0.12)
  other arithmetic: 300 us -> 1.35 us
  waiting for transfers between devices: 253 us -> 12.1 us
  local copies, waits for them, and re-layouts: 233 us -> 2.92 us
  Pallas kernels: 0 us -> 66 us
  starting transfers between devices: 65.8 us -> 22.5 us
  matrix products: 17.6 us -> 0 us
  between operations: 14.1 us -> 0.87 us
    ppermute x22 -> x13, waiting for transfers between devices: 230 us -> 12.1 us  [the longest x3 10.5 us: per_device(): parts.append(lax.ppermute(piece, 'row', pairs))]
    add x11 -> x0, other arithmetic: 171 us -> none  [the longest x10 171 us: smooth(): return current + east_side + north_side]
    slice x51 -> x0, local copies, waits for them, and re-layouts: 125 us -> none  [the longest x20 62 us: smooth(): east_flux = east_weight * (jnp.roll(current, -1, 3) - current)]
    mul x15 -> x0, other arithmetic: 84.4 us -> none  [the longest x10 82.7 us: smooth(): east_flux = east_weight * (jnp.roll(current, -1, 3) - current)]
    pallas_call x0 -> x10, Pallas kernels: none -> 66 us  [the longest x9 64.1 us: run(): return inner(*pinned)]
    while x100 -> x0, local copies, waits for them, and re-layouts: 60.5 us -> none
    ppermute x22 -> x13, starting transfers between devices: 65.7 us -> 22.5 us  [the longest x3 9.57 us: per_device(): second = lax.ppermute(second, 'row', far)]
    concatenate x10 -> x1, other arithmetic: 34.5 us -> 0.01 us  [per_device(): piece = jnp.concatenate([piece, planes], axis=0)]
  transfers between devices with their start and end apart: 23 -> 13, of which waited for: 21 -> 3; matrix products, arithmetic and copies ran while one was open for 2% -> 1% of each run, Pallas kernels for 0% -> 54%
where the time goes in v1:
time: 106 us
  Pallas kernels  66 us (62%)
  starting transfers between devices  22.5 us (21%)
  waiting for transfers between devices  12.1 us (11%)
  local copies, waits for them, and re-layouts  2.92 us (3%)
  other arithmetic  1.35 us (1%)
    pallas_call x9, Pallas kernels, run(): return inner(*pinned)  64.1 us
    ppermute x3, waiting for transfers between devices, per_device(): parts.append(lax.ppermute(piece, 'row', pairs))  10.5 us
    ppermute x3, starting transfers between devices, per_device(): second = lax.ppermute(second, 'row', far)  9.57 us
    ppermute x1, starting transfers between devices, per_device(): other = lax.ppermute(give, 'lev', [(0, 1), (1, 0)])  7.12 us
    ppermute x3, starting transfers between devices, per_device(): parts.append(lax.ppermute(piece, 'row', pairs))  2.84 us
    ppermute x3, starting transfers between devices, per_device(): returned.append(lax.ppermute(sent, 'row', pairs))  2.77 us
  transfers between devices with their start and end apart: 13, of which 3 were waited for; matrix products, arithmetic and copies ran while one was open for 1% of the time, Pallas kernels for 54%

profile of v1, /device:TPU:11, one launch (start us, length us, event | category | flops | bytes accessed | tf_op | source)
XLA Modules:
  0.0 105.7 jit_solution(17152472113194311329)
XLA Ops:
  0.7 1.4 %constant_dynamic-slice_fusion.1 = (bf16[3,8,8,1024]{3,2,1,0:T(8,128)(2,1)S(1)}, bf16[3,8,8,1024]{3,2,1,0:T(8,128)(2,1)S(1)}, bf16[3,8,8,1024]{3,2,1,0:T(8,128)(2,1)S(1)}) fusion(bf16[3,45,8,1024]{3,2,1,0:T(8,128)(2,1)} %fields_ref.1, s32[]{:T(128)} %select_n.48, s32[]{:T(128)S(6)} %select_n.41, s32[]{:T(128)} %select_n.49), kind=kLoop, calls=%fused_computation.17 | loop fusion | bytes 2359308 | tf_op jit(solution)/shard_map/dynamic_slice | solution.py:498
  2.2 1.3 %collective-permute-start.2 = (bf16[28,8,1024]{2,1,0:T(8,128)(2,1)S(1)}, bf16[28,8,1024]{2,1,0:T(8,128)(2,1)S(1)}, u32[]{:S(2)}, u32[]{:S(2)}) collective-permute-start(bf16[28,8,1024]{2,1,0:T(8,128)(2,1)S(1)} %get-tuple-element.64), channel_id=1, source_target_pairs={{0,1},{1,0},{2,3},{3,2},{4,5},{5,4},{6,7},{7,6},{8,9},{9,8},{10,11... | collective-permute-start | bytes 1376264 | tf_op jit(solution)/shard_map/ppermute | solution.py:502
  4.2 5.8 %turn.1 = (bf16[1024,1024]{1,0:T(8,128)(2,1)}, bf16[1024,1024]{1,0:T(8,128)(2,1)}, f32[4,8,1024]{2,1,0:T(8,128)}, bf16[24,8,1024]{2,1,0:T(8,128)(2,1)}, bf16[24,...) custom-call(s32[3]{0:T(128)S(1)} %pad_add_fusion.8.base_ref, bf16[3,45,8,1024]{3,2,1,0:T(8,128)(2,1)} %fields_ref.1, ...), custom_call_target="tpu_custom_call" | custom-call | bytes 73800000 | tf_op jit(solution)/shard_map/turn/pallas_call | solution.py:35
  10.1 3.6 %collective-permute-done.2.part_ref = bf16[28,8,1024]{2,1,0:T(8,128)(2,1)S(1)} collective-permute-done((bf16[28,8,1024]{2,1,0:T(8,128)(2,1)S(1)}, bf16[28,8,1024]{2,1,0:T(8,128)(2,1)S(1)}, u32[]{:S(2)}, u32[]{:S(2)}) %collective-permute-start.2) | collective-permute-done | bytes 458784 | tf_op jit(solution)/shard_map/ppermute | solution.py:502
  13.6 3.8 %gather_rows.3 = (bf16[56,8,1024]{2,1,0:T(8,128)(2,1)}, bf16[35,8,1024]{2,1,0:T(8,128)(2,1)}, bf16[35,8,1024]{2,1,0:T(8,128)(2,1)}) custom-call(s32[2]{0:T(128)S(1)} %pad_add_fusion.7.where_ref, bf16[24,8,1024]{2,1,0:T(8,128)(2,1)} %get-tuple-element.35.own_ref, bf16[28,8,1024]{2,1,0:T(8,128)(2,1)S(1)} %collective-permute-done.2.part_ref, ...), custom_call_target="tpu_custom_call" | custom-call | bytes 73800000 | tf_op jit(solution)/shard_map/gather_rows/pallas_call | solution.py:35
  17.6 4.3 %collective-permute-start.4 = (bf16[35,8,1024]{2,1,0:T(8,128)(2,1)}, bf16[35,8,1024]{2,1,0:T(8,128)(2,1)S(1)}, u32[]{:S(2)}, u32[]{:S(2)}) collective-permute-start(bf16[35,8,1024]{2,1,0:T(8,128)(2,1)} %get-tuple-element.42), channel_id=1, source_target_pairs={{2,4},{3,5},{4,2},{5,3},{10,12},{11,13},{12,10},{13,11},{18,20},{1... | collective-permute-start | bytes 1720328 | tf_op jit(solution)/shard_map/ppermute | solution.py:517
  21.9 1.3 %collective-permute-start.1 = (bf16[24,8,1024]{2,1,0:T(8,128)(2,1)S(1)}, bf16[24,8,1024]{2,1,0:T(8,128)(2,1)S(1)}, u32[]{:S(2)}, u32[]{:S(2)}) collective-permute-start(bf16[24,8,1024]{2,1,0:T(8,128)(2,1)S(1)} %bitcast.42), channel_id=1, source_target_pairs={{0,1},{1,0},{2,3},{3,2},{4,5},{5,4},{6,7},{7,6},{8,9},{9,8},{10,11... | collective-permute-start | bytes 1179656 | tf_op jit(solution)/shard_map/ppermute | solution.py:502
  23.5 7.0 %collective-permute-done.1.part_ref = bf16[24,8,1024]{2,1,0:T(8,128)(2,1)S(1)} collective-permute-done((bf16[24,8,1024]{2,1,0:T(8,128)(2,1)S(1)}, bf16[24,8,1024]{2,1,0:T(8,128)(2,1)S(1)}, u32[]{:S(2)}, u32[]{:S(2)}) %collective-permute-start.1) | collective-permute-done | bytes 393248 | tf_op jit(solution)/shard_map/ppermute | solution.py:502
  30.5 3.7 %gather_rows.4 = (bf16[48,8,1024]{2,1,0:T(8,128)(2,1)}, bf16[30,8,1024]{2,1,0:T(8,128)(2,1)}, bf16[30,8,1024]{2,1,0:T(8,128)(2,1)}) custom-call(s32[2]{0:T(128)S(1)} %pad_add_fusion.7.where_ref, bf16[24,8,1024]{2,1,0:T(8,128)(2,1)} %get-tuple-element.34.own_ref, bf16[24,8,1024]{2,1,0:T(8,128)(2,1)S(1)} %collective-permute-done.1.part_ref, ...), custom_call_target="tpu_custom_call" | custom-call | bytes 73800000 | tf_op jit(solution)/shard_map/gather_rows/pallas_call | solution.py:35
  34.2 2.2 %collective-permute-start.7 = (bf16[30,8,1024]{2,1,0:T(8,128)(2,1)}, bf16[30,8,1024]{2,1,0:T(8,128)(2,1)S(1)}, u32[]{:S(2)}, u32[]{:S(2)}) collective-permute-start(bf16[30,8,1024]{2,1,0:T(8,128)(2,1)} %get-tuple-element.50), channel_id=1, source_target_pairs={{2,4},{3,5},{4,2},{5,3},{10,12},{11,13},{12,10},{13,11},{18,20},{1... | collective-permute-start | bytes 1474568 | tf_op jit(solution)/shard_map/ppermute | solution.py:517
  36.4 11.8 %filter_rows.3 = (f32[4,8,36,128]{3,2,1,0:T(8,128)}, bf16[3,8,8,1024]{3,2,1,0:T(8,128)(2,1)}, bf16[3,8,8,1024]{3,2,1,0:T(8,128)(2,1)}) custom-call(s32[3]{0:T(128)S(1)} %pad_add_fusion.9.refs_0_, bf16[56,8,1024]{2,1,0:T(8,128)(2,1)} %get-tuple-element.41.refs_1_, bf16[35,8,1024]{2,1,0:T(8,128)(2,1)S(1)} %collective-permute-done.3.refs_2_, ...), custom_call_target="tpu_custom_call" | custom-call | bytes 3690000 | tf_op jit(solution)/shard_map/filter_rows/pallas_call | solution.py:35
  48.2 3.7 %gather_rows.5 = (bf16[48,8,1024]{2,1,0:T(8,128)(2,1)}, bf16[30,8,1024]{2,1,0:T(8,128)(2,1)}, bf16[30,8,1024]{2,1,0:T(8,128)(2,1)}) custom-call(s32[2]{0:T(128)S(1)} %pad_add_fusion.7.where_ref, bf16[24,8,1024]{2,1,0:T(8,128)(2,1)} %get-tuple-element.33.own_ref, bf16[24,8,1024]{2,1,0:T(8,128)(2,1)S(1)} %collective-permute-done.part_ref, ...), custom_call_target="tpu_custom_call" | custom-call | bytes 73800000 | tf_op jit(solution)/shard_map/gather_rows/pallas_call | solution.py:35
  52.0 3.1 %collective-permute-start.9 = (bf16[30,8,1024]{2,1,0:T(8,128)(2,1)}, bf16[30,8,1024]{2,1,0:T(8,128)(2,1)S(1)}, u32[]{:S(2)}, u32[]{:S(2)}) collective-permute-start(bf16[30,8,1024]{2,1,0:T(8,128)(2,1)} %get-tuple-element.55), channel_id=1, source_target_pairs={{2,4},{3,5},{4,2},{5,3},{10,12},{11,13},{12,10},{13,11},{18,20},{1... | collective-permute-start | bytes 1474568 | tf_op jit(solution)/shard_map/ppermute | solution.py:517
  55.1 1.3 %collective-permute-start.8 = (bf16[3,8,8,1024]{3,2,1,0:T(8,128)(2,1)S(1)}, bf16[3,8,8,1024]{3,2,1,0:T(8,128)(2,1)S(1)}, u32[]{:S(2)}, u32[]{:S(2)}) collective-permute-start(bf16[3,8,8,1024]{3,2,1,0:T(8,128)(2,1)S(1)} %copy-done.6), channel_id=1, source_target_pairs={{0,1},{1,0},{2,3},{3,2},{4,5},{5,4},{6,7},{7,6},{8,9},{9,8},{10,11... | collective-permute-start | bytes 1179656 | tf_op jit(solution)/shard_map/ppermute | solution.py:527
  56.5 11.9 %filter_rows.4 = (bf16[3,8,8,1024]{3,2,1,0:T(8,128)(2,1)}, bf16[3,8,8,1024]{3,2,1,0:T(8,128)(2,1)}) custom-call(s32[3]{0:T(128)S(1)} %pad_add_fusion.10.refs_0_, bf16[48,8,1024]{2,1,0:T(8,128)(2,1)} %get-tuple-element.48.refs_1_, bf16[30,8,1024]{2,1,0:T(8,128)(2,1)S(1)} %collective-permute-done.6.refs_2_, ...), custom_call_target="tpu_custom_call" | custom-call | bytes 3690000 | tf_op jit(solution)/shard_map/filter_rows/pallas_call | solution.py:35
  68.7 11.8 %filter_rows.5 = (bf16[3,8,8,1024]{3,2,1,0:T(8,128)(2,1)}, bf16[3,8,8,1024]{3,2,1,0:T(8,128)(2,1)}) custom-call(s32[3]{0:T(128)S(1)} %pad_add_fusion.5.refs_0_, bf16[48,8,1024]{2,1,0:T(8,128)(2,1)} %get-tuple-element.46.refs_1_, bf16[30,8,1024]{2,1,0:T(8,128)(2,1)S(1)} %collective-permute-done.5.refs_2_, ...), custom_call_target="tpu_custom_call" | custom-call | bytes 3690000 | tf_op jit(solution)/shard_map/filter_rows/pallas_call | solution.py:35
  80.5 1.2 %collective-permute-start.10 = (bf16[3,8,8,1024]{3,2,1,0:T(8,128)(2,1)}, bf16[3,8,8,1024]{3,2,1,0:T(8,128)(2,1)S(1)}, u32[]{:S(2)}, u32[]{:S(2)}) collective-permute-start(bf16[3,8,8,1024]{3,2,1,0:T(8,128)(2,1)} %get-tuple-element.56), channel_id=1, source_target_pairs={{0,1},{1,0},{2,3},{3,2},{4,5},{5,4},{6,7},{7,6},{8,9},{9,8},{10,11... | collective-permute-start | bytes 1179656 | tf_op jit(solution)/shard_map/ppermute | solution.py:527
  82.1 0.7 copy-done.1
  82.8 7.9 %project.2 = (bf16[3,45,8,1024]{3,2,1,0:T(8,128)(2,1)}, f32[3,8,8,1024]{3,2,1,0:T(8,128)}) custom-call(s32[5,2]{1,0:T(8,128)S(1)} %stack.153.refs_0_, bf16[3,8,8,1024]{3,2,1,0:T(8,128)(2,1)} %get-tuple-element.44.refs_1_, bf16[3,8,8,1024]{3,2,1,0:T(8,128)(2,1)} %get-tuple-element.52.refs_2_, bf16[3,8,8,1024]{3,2,1,0:T(8,128)(2,1)} %get-tuple-element.57.refs_3_, ...), custom_call_target="tpu_custom_call" | custom-call | bytes 73800000 | tf_op jit(solution)/shard_map/project/pallas_call | solution.py:35
  90.7 3.7 %project.3 = (bf16[3,45,8,1024]{3,2,1,0:T(8,128)(2,1)}, f32[3,8,8,512]{3,2,1,0:T(8,128)}, f32[3,8,8,512]{3,2,1,0:T(8,128)}) custom-call(s32[1,3]{1,0:T(1,128)S(1)} %add_bitcast_fusion.refs_0_, bf16[3,8,8,1024]{3,2,1,0:T(8,128)(2,1)S(1)} %collective-permute-done.10.refs_1_, bf16[8,45,8,1024]{3,2,1,0:T(8,128)(2,1)} %refs_2_.1, ...), custom_call_target="tpu_custom_call", output_to_operand_aliasing={{0}: (4, {})} | custom-call | bytes 73800000 | tf_op jit(solution)/shard_map/project/pallas_call | solution.py:35
  94.4 7.1 %collective-permute-start.12 = (f32[3,8,8,512]{3,2,1,0:T(8,128)}, f32[3,8,8,512]{3,2,1,0:T(8,128)S(1)}, u32[]{:S(2)}, u32[]{:S(2)}) collective-permute-start(f32[3,8,8,512]{3,2,1,0:T(8,128)} %get-tuple-element.63), channel_id=1, source_target_pairs={{0,8},{8,0},{1,9},{9,1},{2,10},{10,2},{3,11},{11,3},{4,12},{12,4},... | collective-permute-start | bytes 1179656 | tf_op jit(solution)/shard_map/ppermute | solution.py:550
  101.5 1.6 %collective-permute-done.12.other_ref = f32[3,8,8,512]{3,2,1,0:T(8,128)S(1)} collective-permute-done((f32[3,8,8,512]{3,2,1,0:T(8,128)}, f32[3,8,8,512]{3,2,1,0:T(8,128)S(1)}, u32[]{:S(2)}, u32[]{:S(2)}) %collective-permute-start.12) | collective-permute-done | bytes 393248 | tf_op jit(solution)/shard_map/ppermute | solution.py:550
  103.1 0.7 copy-done.2
  103.8 1.9 %flux.1 = f32[3,8,8,512]{3,2,1,0:T(8,128)} custom-call(f32[3,8,8,512]{3,2,1,0:T(8,128)} %get-tuple-element.62.keep_ref, f32[3,8,8,512]{3,2,1,0:T(8,128)} %copy-done.2), custom_call_target="tpu_custom_call" | custom-call | tf_op jit(solution)/shard_map/flux/pallas_call | solution.py:551
  (43 shorter events, 2.1 us)
Async XLA Ops:
  0.6 1.5 %copy-start.3 = (f32[8,1024]{1,0:T(8,128)S(1)}, f32[8,1024]{1,0:T(8,128)}, u32[]{:S(2)}) copy-start(f32[8,1024]{1,0:T(8,128)} %param.7) | copy-start | bytes 98308
  0.6 1.5 %copy-start.4 = (s32[8,1024]{1,0:T(8,128)S(1)}, s32[8,1024]{1,0:T(8,128)}, u32[]{:S(2)}) copy-start(s32[8,1024]{1,0:T(8,128)} %param.8) | copy-start | bytes 98308
  0.7 1.5 %copy-start.5 = (s32[8,1024]{1,0:T(8,128)S(1)}, s32[8,1024]{1,0:T(8,128)}, u32[]{:S(2)}) copy-start(s32[8,1024]{1,0:T(8,128)} %param.9) | copy-start | bytes 98308
  2.2 11.5 %collective-permute-start.2 = (bf16[28,8,1024]{2,1,0:T(8,128)(2,1)S(1)}, bf16[28,8,1024]{2,1,0:T(8,128)(2,1)S(1)}, u32[]{:S(2)}, u32[]{:S(2)}) collective-permute-start(bf16[28,8,1024]{2,1,0:T(8,128)(2,1)S(1)} %get-tuple-element.64), channel_id=1, source_target_pairs={{0,1},{1,0},{2,3},{3,2},{4,5},{5,4},{6,7},{7,6},{8,9},{9,8},{10,11... | collective-permute-start | bytes 1376264 | tf_op jit(solution)/shard_map/ppermute | solution.py:502
  17.4 19.0 %collective-permute-start.3 = (bf16[35,8,1024]{2,1,0:T(8,128)(2,1)}, bf16[35,8,1024]{2,1,0:T(8,128)(2,1)S(1)}, u32[]{:S(2)}, u32[]{:S(2)}) collective-permute-start(bf16[35,8,1024]{2,1,0:T(8,128)(2,1)} %get-tuple-element.38), channel_id=1, source_target_pairs={{0,2},{1,3},{2,0},{3,1},{4,6},{5,7},{6,4},{7,5},{8,10},{9,11},{10,... | collective-permute-start | bytes 1720328 | tf_op jit(solution)/shard_map/ppermute | solution.py:516
  17.6 18.8 %collective-permute-start.4 = (bf16[35,8,1024]{2,1,0:T(8,128)(2,1)}, bf16[35,8,1024]{2,1,0:T(8,128)(2,1)S(1)}, u32[]{:S(2)}, u32[]{:S(2)}) collective-permute-start(bf16[35,8,1024]{2,1,0:T(8,128)(2,1)} %get-tuple-element.42), channel_id=1, source_target_pairs={{2,4},{3,5},{4,2},{5,3},{10,12},{11,13},{12,10},{13,11},{18,20},{1... | collective-permute-start | bytes 1720328 | tf_op jit(solution)/shard_map/ppermute | solution.py:517
  21.9 8.6 %collective-permute-start.1 = (bf16[24,8,1024]{2,1,0:T(8,128)(2,1)S(1)}, bf16[24,8,1024]{2,1,0:T(8,128)(2,1)S(1)}, u32[]{:S(2)}, u32[]{:S(2)}) collective-permute-start(bf16[24,8,1024]{2,1,0:T(8,128)(2,1)S(1)} %bitcast.42), channel_id=1, source_target_pairs={{0,1},{1,0},{2,3},{3,2},{4,5},{5,4},{6,7},{7,6},{8,9},{9,8},{10,11... | collective-permute-start | bytes 1179656 | tf_op jit(solution)/shard_map/ppermute | solution.py:502
  23.2 25.0 %collective-permute-start = (bf16[24,8,1024]{2,1,0:T(8,128)(2,1)S(1)}, bf16[24,8,1024]{2,1,0:T(8,128)(2,1)S(1)}, u32[]{:S(2)}, u32[]{:S(2)}) collective-permute-start(bf16[24,8,1024]{2,1,0:T(8,128)(2,1)S(1)} %bitcast.41), channel_id=1, source_target_pairs={{0,1},{1,0},{2,3},{3,2},{4,5},{5,4},{6,7},{7,6},{8,9},{9,8},{10,11... | collective-permute-start | bytes 1179656 | tf_op jit(solution)/shard_map/ppermute | solution.py:502
  34.2 22.3 %collective-permute-start.6 = (bf16[30,8,1024]{2,1,0:T(8,128)(2,1)}, bf16[30,8,1024]{2,1,0:T(8,128)(2,1)S(1)}, u32[]{:S(2)}, u32[]{:S(2)}) collective-permute-start(bf16[30,8,1024]{2,1,0:T(8,128)(2,1)} %get-tuple-element.40), channel_id=1, source_target_pairs={{0,2},{1,3},{2,0},{3,1},{4,6},{5,7},{6,4},{7,5},{8,10},{9,11},{10,... | collective-permute-start | bytes 1474568 | tf_op jit(solution)/shard_map/ppermute | solution.py:516
  34.2 22.3 %collective-permute-start.7 = (bf16[30,8,1024]{2,1,0:T(8,128)(2,1)}, bf16[30,8,1024]{2,1,0:T(8,128)(2,1)S(1)}, u32[]{:S(2)}, u32[]{:S(2)}) collective-permute-start(bf16[30,8,1024]{2,1,0:T(8,128)(2,1)} %get-tuple-element.50), channel_id=1, source_target_pairs={{2,4},{3,5},{4,2},{5,3},{10,12},{11,13},{12,10},{13,11},{18,20},{1... | collective-permute-start | bytes 1474568 | tf_op jit(solution)/shard_map/ppermute | solution.py:517
  48.2 6.8 %copy-start.6 = (bf16[3,8,8,1024]{3,2,1,0:T(8,128)(2,1)S(1)}, bf16[3,8,8,1024]{3,2,1,0:T(8,128)(2,1)}, u32[]{:S(2)}) copy-start(bf16[3,8,8,1024]{3,2,1,0:T(8,128)(2,1)} %get-tuple-element.53) | copy-start | bytes 1179652
  52.0 16.7 %collective-permute-start.5 = (bf16[30,8,1024]{2,1,0:T(8,128)(2,1)}, bf16[30,8,1024]{2,1,0:T(8,128)(2,1)S(1)}, u32[]{:S(2)}, u32[]{:S(2)}) collective-permute-start(bf16[30,8,1024]{2,1,0:T(8,128)(2,1)} %get-tuple-element.47), channel_id=1, source_target_pairs={{0,2},{1,3},{2,0},{3,1},{4,6},{5,7},{6,4},{7,5},{8,10},{9,11},{10,... | collective-permute-start | bytes 1474568 | tf_op jit(solution)/shard_map/ppermute | solution.py:516
  52.0 16.7 %collective-permute-start.9 = (bf16[30,8,1024]{2,1,0:T(8,128)(2,1)}, bf16[30,8,1024]{2,1,0:T(8,128)(2,1)S(1)}, u32[]{:S(2)}, u32[]{:S(2)}) collective-permute-start(bf16[30,8,1024]{2,1,0:T(8,128)(2,1)} %get-tuple-element.55), channel_id=1, source_target_pairs={{2,4},{3,5},{4,2},{5,3},{10,12},{11,13},{12,10},{13,11},{18,20},{1... | collective-permute-start | bytes 1474568 | tf_op jit(solution)/shard_map/ppermute | solution.py:517
  55.1 13.6 %collective-permute-start.8 = (bf16[3,8,8,1024]{3,2,1,0:T(8,128)(2,1)S(1)}, bf16[3,8,8,1024]{3,2,1,0:T(8,128)(2,1)S(1)}, u32[]{:S(2)}, u32[]{:S(2)}) collective-permute-start(bf16[3,8,8,1024]{3,2,1,0:T(8,128)(2,1)S(1)} %copy-done.6), channel_id=1, source_target_pairs={{0,1},{1,0},{2,3},{3,2},{4,5},{5,4},{6,7},{7,6},{8,9},{9,8},{10,11... | collective-permute-start | bytes 1179656 | tf_op jit(solution)/shard_map/ppermute | solution.py:527
  68.4 13.7 %collective-permute-start.11 = (bf16[3,8,8,1024]{3,2,1,0:T(8,128)(2,1)}, bf16[3,8,8,1024]{3,2,1,0:T(8,128)(2,1)S(1)}, u32[]{:S(2)}, u32[]{:S(2)}) collective-permute-start(bf16[3,8,8,1024]{3,2,1,0:T(8,128)(2,1)} %get-tuple-element.58), channel_id=1, source_target_pairs={{0,1},{1,0},{2,3},{3,2},{4,5},{5,4},{6,7},{7,6},{8,9},{9,8},{10,11... | collective-permute-start | bytes 1179656 | tf_op jit(solution)/shard_map/ppermute | solution.py:527
  68.6 11.9 %copy-start = (bf16[3,8,8,1024]{3,2,1,0:T(8,128)(2,1)}, bf16[3,8,8,1024]{3,2,1,0:T(8,128)(2,1)S(1)}, u32[]{:S(2)}) copy-start(bf16[3,8,8,1024]{3,2,1,0:T(8,128)(2,1)S(1)} %collective-permute-done.8.refs_4_) | copy-start | bytes 1179652
  80.5 10.2 %collective-permute-start.10 = (bf16[3,8,8,1024]{3,2,1,0:T(8,128)(2,1)}, bf16[3,8,8,1024]{3,2,1,0:T(8,128)(2,1)S(1)}, u32[]{:S(2)}, u32[]{:S(2)}) collective-permute-start(bf16[3,8,8,1024]{3,2,1,0:T(8,128)(2,1)} %get-tuple-element.56), channel_id=1, source_target_pairs={{0,1},{1,0},{2,3},{3,2},{4,5},{5,4},{6,7},{7,6},{8,9},{9,8},{10,11... | collective-permute-start | bytes 1179656 | tf_op jit(solution)/shard_map/ppermute | solution.py:527
  82.1 0.7 copy-start.1
  94.4 8.7 %collective-permute-start.12 = (f32[3,8,8,512]{3,2,1,0:T(8,128)}, f32[3,8,8,512]{3,2,1,0:T(8,128)S(1)}, u32[]{:S(2)}, u32[]{:S(2)}) collective-permute-start(f32[3,8,8,512]{3,2,1,0:T(8,128)} %get-tuple-element.63), channel_id=1, source_target_pairs={{0,8},{8,0},{1,9},{9,1},{2,10},{10,2},{3,11},{11,3},{4,12},{12,4},... | collective-permute-start | bytes 1179656 | tf_op jit(solution)/shard_map/ppermute | solution.py:550
  103.1 0.7 copy-start.2

commit v2 on v1

--- a/solution.py
+++ b/solution.py
@@ -42,7 +42,7 @@
 
 
 def cost(us):
-    return pl.CostEstimate(flops=0, transcendentals=0, bytes_accessed=us * 3_690_000)
+    return pl.CostEstimate(flops=us * 1_150_000_000, transcendentals=0, bytes_accessed=us * 3_690_000)
 
 
 def spread_fill(spread_ref, unspread_ref):
@@ -220,13 +220,24 @@
         face_ref[3, j] = jnp.minimum(here[1], north[1])
 
 
-def filter_body(leads, scal_ref, pair_ref, first_ref, second_ref, back_ref, *refs):
-    face_ref, mine_ref, send_ref = refs[:3]
+def filter_body(leads, sent, scal_ref, pair_hbm, first_ref, second_ref, back_hbm, *refs):
+    face_hbm, mine_hbm, send_hbm = refs[:3]
     cur_ref, east_ref, west_ref, north_ref, turn_ref = refs[3:8]
+    pair_ref, back_ref, face_ref, out_ref, sems = refs[8:13]
+    planes_ref, spare_ref = refs[13:] if leads else (None, None)
     fields, total, tiles, _, _ = cur_ref.shape
     cols = tiles * LANES
     pair = total - 2 * ITERS
     rows = pair // 2
+    get_pair = pltpu.make_async_copy(pair_hbm, pair_ref, sems.at[0])
+    get_back = pltpu.make_async_copy(back_hbm, back_ref, sems.at[1])
+    if leads:
+        move_face = pltpu.make_async_copy(face_ref, face_hbm, sems.at[2])
+    else:
+        move_face = pltpu.make_async_copy(face_hbm, face_ref, sems.at[2])
+        move_face.start()
+    get_pair.start()
+    get_back.start()
     side = scal_ref[0]
     level = (scal_ref[2] + lax.broadcasted_iota(jnp.int32, (GROUP, LANES), 0)).astype(F32)
 
@@ -237,7 +248,6 @@
                     value = src[r * fields + f, :, pl.ds(j * LANES, LANES)]
                     cur_ref[f, dst_row + r, j] = value.astype(F32)
         if leads:
-            planes_ref = refs[8]
             block = count * PLANES
             for j in range(tiles):
                 value = src[pl.ds(count * fields, block // GROUP), :, pl.ds(j * LANES, LANES)]
@@ -255,9 +265,13 @@
         fill(first_ref, 0, ITERS)
         fill(second_ref, ITERS + pair, ITERS)
 
+    if not leads:
+        move_face.wait()
+    get_pair.wait()
     fill(pair_ref, ITERS, pair)
     if leads:
-        make_faces(face_ref, refs[8], refs[9])
+        make_faces(face_ref, planes_ref, spare_ref)
+        move_face.start()
 
     def weights(r, _):
         for j in range(tiles):
@@ -298,21 +312,33 @@
 
     lax.fori_loop(0, fields, one_field, 0)
 
-    def emit(dst, start):
+    block = fields * GROUP * rows
+    starts = (ITERS + rows * (1 - side), ITERS + rows * side)
+    for n, start in enumerate(starts):
         for f in range(fields):
             for r in range(rows):
                 for j in range(tiles):
-                    spots = pl.ds(f * GROUP * rows + r, GROUP, stride=rows)
+                    spots = pl.ds(n * block + f * GROUP * rows + r, GROUP, stride=rows)
                     turn_ref[j, spots, :] = cur_ref[f, start + r, j]
-        flat = jnp.concatenate([turn_ref[j].astype(BF16) for j in range(tiles)], axis=1)
-        moved = jnp.dot(flat, back_ref[...], preferred_element_type=F32)
-        dst[...] = moved.reshape(fields, GROUP, rows, cols).astype(BF16)
-
-    emit(send_ref, ITERS + rows * (1 - side))
-    emit(mine_ref, ITERS + rows * side)
-
-
-def filter_rows(scalars, pair, first, second, unspread, faces, fields, rows):
+    get_back.wait()
+    flat = jnp.concatenate([turn_ref[j].astype(BF16) for j in range(tiles)], axis=1)
+    moved = jnp.dot(flat, back_ref[...], preferred_element_type=F32)
+    puts = []
+    for n, dst in enumerate((send_hbm, mine_hbm)):
+        value = moved[n * block : (n + 1) * block]
+        out_ref[n] = value.reshape(fields, GROUP, rows, cols).astype(BF16)
+        src = out_ref.at[n]
+        if n == 0 and sent < GROUP:
+            src = src.at[:, pl.ds(side * (GROUP - sent), sent)]
+        puts.append(pltpu.make_async_copy(src, dst, sems.at[3 + n]))
+        puts[-1].start()
+    for put in puts:
+        put.wait()
+    if leads:
+        move_face.wait()
+
+
+def filter_rows(scalars, pair, first, second, unspread, faces, fields, rows, sent):
     cols = pair.shape[2]
     total = 2 * rows + 2 * ITERS
     tiles = cols // LANES
@@ -324,7 +350,12 @@
         pltpu.VMEM((total, tiles, GROUP, LANES), F32),
         pltpu.VMEM((total, GROUP, LANES), F32),
         pltpu.VMEM((total, tiles, GROUP, LANES), F32),
-        pltpu.VMEM((tiles, fields * GROUP * rows, LANES), F32),
+        pltpu.VMEM((tiles, 2 * fields * GROUP * rows, LANES), F32),
+        pltpu.VMEM(pair.shape, BF16),
+        pltpu.VMEM((cols, cols), BF16),
+        pltpu.VMEM(face.shape, F32),
+        pltpu.VMEM((2,) + out.shape, BF16),
+        pltpu.SemaphoreType.DMA((5,)),
     ]
     if leads:
         spare = -(-(total + 1) // GROUP) * GROUP
@@ -334,16 +365,16 @@
         ]
 
     def body(*refs):
-        filter_body(leads, *refs)
+        filter_body(leads, sent, *refs)
 
     return call(
         body,
         landed=(2, 3),
-        out_shape=((face,) if leads else ()) + (out, out),
-        in_specs=[whole(pltpu.SMEM)]
-        + [whole()] * 4
-        + ([] if leads else [whole()]),
-        out_specs=(whole(),) * (3 if leads else 2),
+        out_shape=((face,) if leads else ())
+        + (out, jax.ShapeDtypeStruct((fields, sent, rows, cols), BF16)),
+        in_specs=[whole(pltpu.SMEM), whole(pl.ANY), whole(), whole(), whole(pl.ANY)]
+        + ([] if leads else [whole(pl.ANY)]),
+        out_specs=(whole(pl.ANY),) * (3 if leads else 2),
         scratch_shapes=scratch,
         compiler_params=params(24),
         cost_estimate=cost(FILTER_COST),
@@ -368,7 +399,8 @@
     else:
         amp_ref = refs.pop(0)
     mode_bufs = refs[:count]
-    out_sems, mode_sems = refs[count:]
+    out_sems, mode_sems, chunk_sems = refs[count : count + 3]
+    spare = refs[count + 3 :]
     fields, _, rows, cols = chunk_refs[0].shape
     modes = modes_ref.shape[0]
     fetches = [
@@ -377,19 +409,34 @@
         )
         for n in range(count)
     ]
+    if has_start:
+        chunk_bufs = chunk_refs
+        loads = [pltpu.make_async_copy(start_ref, spare[0], chunk_sems.at[0])]
+        start_ref = spare[0]
+    else:
+        chunk_bufs = spare
+        loads = [
+            pltpu.make_async_copy(chunk_refs[n], chunk_bufs[n], chunk_sems.at[n])
+            for n in range(count)
+        ]
     copies = [
         pltpu.make_async_copy(
-            chunk_refs[n].at[:, pl.ds(base_ref[n, 1], takes[n])],
+            chunk_bufs[n].at[:, pl.ds(base_ref[n, 1], takes[n])],
             out_ref.at[:, pl.ds(base_ref[n, 0], takes[n])],
             out_sems.at[n],
         )
         for n in range(count)
     ]
+    for load in loads:
+        load.start()
+    if has_start:
+        copies[0].start()
     for fetch in fetches:
         fetch.start()
-    for copy in copies:
-        copy.start()
     for n in range(count):
+        loads[n].wait()
+        if not has_start:
+            copies[n].start()
         fetches[n].wait()
 
         def one_tile(tile, dst, dst_tile, _):
@@ -406,7 +453,7 @@
                         sums.append(jnp.zeros((rows, LANES), F32))
             for i in range(takes[n]):
                 values = [
-                    chunk_refs[n][f, base_ref[n, 1] + i, :, lanes].astype(F32)
+                    chunk_bufs[n][f, base_ref[n, 1] + i, :, lanes].astype(F32)
                     for f in range(fields)
                 ]
                 for k in range(modes):
@@ -447,13 +494,18 @@
         out_shape=(jax.ShapeDtypeStruct((fields, levels, rows, cols), BF16),)
         + (amplitude,) * halves,
         in_specs=[whole(pltpu.SMEM)]
-        + [whole()] * count
+        + [whole() if carried else whole(pl.ANY)] * count
         + [whole(pl.ANY)]
-        + ([whole(), whole(pl.ANY)] if carried else []),
+        + ([whole(pl.ANY), whole(pl.ANY)] if carried else []),
         out_specs=(whole(pl.ANY),) + (whole(),) * halves,
         input_output_aliases={count + 3: 0} if carried else {},
         scratch_shapes=[pltpu.VMEM((modes, take, rows, cols), BF16) for take in takes]
-        + [pltpu.SemaphoreType.DMA((count,))] * 2,
+        + [pltpu.SemaphoreType.DMA((count,))] * 3
+        + (
+            [pltpu.VMEM((fields, modes, rows, cols), F32)]
+            if carried
+            else [pltpu.VMEM(chunk.shape, BF16) for chunk in chunks]
+        ),
         compiler_params=params(24),
         cost_estimate=cost(PROJECT_COST),
         name="project",
@@ -502,13 +554,15 @@
         parts.append(lax.ppermute(piece, "row", pairs))
     spread, unspread, statics, *owns = turn(ours, fields, planes)
 
+    cut = levels - (2 * chunks - 1) * GROUP
+    skip = jnp.where(side == 0, GROUP - cut, 0).astype(jnp.int32)
     where = jnp.stack([side, odd])
     mine, returned, edges = ([], [], [])
     faces = None
     for c in range(chunks):
         part = parts[c]
         if c > 0:
-            part, *_ = lax.optimization_barrier((part, edges[-1], mine[: c - 1]))
+            part, *_ = lax.optimization_barrier((part, edges[-1]))
         pair, first, second = gather_rows(
             where, owns[c], part, spread, statics if c == 0 else None
         )
@@ -517,17 +571,16 @@
         second = lax.ppermute(second, "row", far)
         if c > 0:
             first, *_ = lax.optimization_barrier((first, mine[-1], returned[: c - 1]))
+        sent = GROUP if c + 1 < chunks else cut
         scalars = jnp.stack([side, odd, lev * levels + ours[c]])
-        *lead, kept, sent = filter_rows(
-            scalars, pair, first, second, unspread, faces, count, rows
+        *lead, kept, gone = filter_rows(
+            scalars, pair, first, second, unspread, faces, count, rows, sent
         )
         if c == 0:
             faces = lead[0]
         mine.append(kept)
-        returned.append(lax.ppermute(sent, "row", pairs))
-
-    cut = levels - (2 * chunks - 1) * GROUP
-    first = jnp.where(side == 0, GROUP - cut, 0).astype(jnp.int32)
+        returned.append(lax.ppermute(gone, "row", pairs))
+
     zero = jnp.zeros((), jnp.int32)
     bases = [jnp.stack([b, zero]) for b in ours + theirs[:-1]]
     filtered, amplitude = project(
@@ -539,7 +592,7 @@
         1,
     )
     filtered, keep, give = project(
-        jnp.stack([theirs[-1] + first, first, lev])[None],
+        jnp.stack([theirs[-1] + skip, zero, lev])[None],
         returned[-1:],
         [cut],
         vertical_modes,
@@ -548,8 +601,13 @@
         (amplitude, filtered),
     )
     other = lax.ppermute(give, "lev", [(0, 1), (1, 0)])
-    modal_flux = pl.pallas_call(
-        flux_body, out_shape=jax.ShapeDtypeStruct(keep.shape, F32), name="flux"
+    (modal_flux,) = call(
+        flux_body,
+        landed=(1,),
+        out_shape=(jax.ShapeDtypeStruct(keep.shape, F32),),
+        in_specs=[whole(), whole()],
+        out_specs=(whole(),),
+        name="flux",
     )(keep, other)
     return (filtered, modal_flux)
 

time: 106 us -> 94.8 us (0.89)
  waiting for transfers between devices: 12.1 us -> 3.66 us
  Pallas kernels: 66 us -> 64.1 us
    ppermute x3, waiting for transfers between devices: 10.5 us -> 2.07 us  [per_device(): parts.append(lax.ppermute(piece, 'row', pairs))]
    ppermute x1, starting transfers between devices: 7.12 us -> 3.01 us  [per_device(): other = lax.ppermute(give, 'lev', [(0, 1), (1, 0)])]
    ppermute x3, starting transfers between devices: 9.57 us -> 13 us  [per_device(): second = lax.ppermute(second, 'row', far)]
    pallas_call x1 -> x0, Pallas kernels: 1.91 us -> none  [per_device(): pl.pallas_call(flux_body, out_shape=jax.ShapeDtypeStruct(keep.shape, F32)...]
    pallas_call x9 -> x10, Pallas kernels: 64.1 us -> 64.1 us  [run(): return inner(*pinned)]
  transfers between devices with their start and end apart: 13 -> 13, of which waited for: 3 -> 3; matrix products, arithmetic and copies ran while one was open for 1% -> 1% of each run, Pallas kernels for 54% -> 63%
where the time goes in v2:
time: 94.8 us; the launch traced here: 94.3 us
  Pallas kernels  64.1 us (68%)
  starting transfers between devices  22.2 us (23%)
  waiting for transfers between devices  3.66 us (4%)
  local copies, waits for them, and re-layouts  2.18 us (2%)
  other arithmetic  1.33 us (1%)
    pallas_call x10, Pallas kernels, run(): return inner(*pinned)  64.1 us
    ppermute x3, starting transfers between devices, per_device(): second = lax.ppermute(second, 'row', far)  13 us
    ppermute x1, starting transfers between devices, per_device(): other = lax.ppermute(give, 'lev', [(0, 1), (1, 0)])  3.01 us
    ppermute x3, starting transfers between devices, per_device(): returned.append(lax.ppermute(gone, 'row', pairs))  2.9 us
    ppermute x3, starting transfers between devices, per_device(): parts.append(lax.ppermute(piece, 'row', pairs))  2.77 us
    ppermute x3, waiting for transfers between devices, per_device(): parts.append(lax.ppermute(piece, 'row', pairs))  2.07 us
  transfers between devices with their start and end apart: 13, of which 3 were waited for; matrix products, arithmetic and copies ran while one was open for 1% of the time, Pallas kernels for 63%

profile of v2, /device:TPU:11, one launch (start us, length us, event | category | flops | bytes accessed | tf_op | source)
XLA Modules:
  0.0 94.3 jit_solution(3191272539514728840)
XLA Ops:
  0.7 1.3 %constant_dynamic-slice_fusion.1 = (bf16[3,8,8,1024]{3,2,1,0:T(8,128)(2,1)S(1)}, bf16[3,8,8,1024]{3,2,1,0:T(8,128)(2,1)S(1)}, bf16[3,8,8,1024]{3,2,1,0:T(8,128)(2,1)S(1)}) fusion(bf16[3,45,8,1024]{3,2,1,0:T(8,128)(2,1)} %fields_ref.1, s32[]{:T(128)} %select_n.48, s32[]{:T(128)S(6)} %select_n.41, s32[]{:T(128)} %select_n.49), kind=kLoop, calls=%fused_computation.17 | loop fusion | bytes 2359308 | tf_op jit(solution)/shard_map/dynamic_slice | solution.py:550
  2.2 1.3 %collective-permute-start.2 = (bf16[28,8,1024]{2,1,0:T(8,128)(2,1)S(1)}, bf16[28,8,1024]{2,1,0:T(8,128)(2,1)S(1)}, u32[]{:S(2)}, u32[]{:S(2)}) collective-permute-start(bf16[28,8,1024]{2,1,0:T(8,128)(2,1)S(1)} %get-tuple-element.64), channel_id=1, source_target_pairs={{0,1},{1,0},{2,3},{3,2},{4,5},{5,4},{6,7},{7,6},{8,9},{9,8},{10,11... | collective-permute-start | bytes 1376264 | tf_op jit(solution)/shard_map/ppermute | solution.py:554
  3.7 1.2 %collective-permute-start = (bf16[24,8,1024]{2,1,0:T(8,128)(2,1)S(1)}, bf16[24,8,1024]{2,1,0:T(8,128)(2,1)S(1)}, u32[]{:S(2)}, u32[]{:S(2)}) collective-permute-start(bf16[24,8,1024]{2,1,0:T(8,128)(2,1)S(1)} %bitcast.40), channel_id=1, source_target_pairs={{0,1},{1,0},{2,3},{3,2},{4,5},{5,4},{6,7},{7,6},{8,9},{9,8},{10,11... | collective-permute-start | bytes 1179656 | tf_op jit(solution)/shard_map/ppermute | solution.py:554
  5.0 0.6 pad_maximum_fusion.planes_ref
  5.6 5.8 %turn.1 = (bf16[1024,1024]{1,0:T(8,128)(2,1)}, bf16[1024,1024]{1,0:T(8,128)(2,1)}, f32[4,8,1024]{2,1,0:T(8,128)}, bf16[24,8,1024]{2,1,0:T(8,128)(2,1)}, bf16[24,...) custom-call(s32[3]{0:T(128)S(1)} %pad_add_fusion.8.base_ref, bf16[3,45,8,1024]{3,2,1,0:T(8,128)(2,1)} %fields_ref.1, ...), custom_call_target="tpu_custom_call" | custom-call | flops 23000000512 | bytes 73800000 | tf_op jit(solution)/shard_map/turn/pallas_call | solution.py:35
  11.8 1.8 %collective-permute-done.2.part_ref = bf16[28,8,1024]{2,1,0:T(8,128)(2,1)S(1)} collective-permute-done((bf16[28,8,1024]{2,1,0:T(8,128)(2,1)S(1)}, bf16[28,8,1024]{2,1,0:T(8,128)(2,1)S(1)}, u32[]{:S(2)}, u32[]{:S(2)}) %collective-permute-start.2) | collective-permute-done | bytes 458784 | tf_op jit(solution)/shard_map/ppermute | solution.py:554
  13.6 3.9 %gather_rows.3 = (bf16[56,8,1024]{2,1,0:T(8,128)(2,1)}, bf16[35,8,1024]{2,1,0:T(8,128)(2,1)}, bf16[35,8,1024]{2,1,0:T(8,128)(2,1)}) custom-call(s32[2]{0:T(128)S(1)} %pad_add_fusion.7.where_ref, bf16[24,8,1024]{2,1,0:T(8,128)(2,1)} %get-tuple-element.35.own_ref, bf16[28,8,1024]{2,1,0:T(8,128)(2,1)S(1)} %collective-permute-done.2.part_ref, ...), custom_call_target="tpu_custom_call" | custom-call | flops 23000000512 | bytes 73800000 | tf_op jit(solution)/shard_map/gather_rows/pallas_call | solution.py:35
  17.7 4.3 %collective-permute-start.6 = (bf16[35,8,1024]{2,1,0:T(8,128)(2,1)}, bf16[35,8,1024]{2,1,0:T(8,128)(2,1)S(1)}, u32[]{:S(2)}, u32[]{:S(2)}) collective-permute-start(bf16[35,8,1024]{2,1,0:T(8,128)(2,1)} %get-tuple-element.46), channel_id=1, source_target_pairs={{2,4},{3,5},{4,2},{5,3},{10,12},{11,13},{12,10},{13,11},{18,20},{1... | collective-permute-start | bytes 1720328 | tf_op jit(solution)/shard_map/ppermute | solution.py:571
  22.0 3.7 %gather_rows.4 = (bf16[48,8,1024]{2,1,0:T(8,128)(2,1)}, bf16[30,8,1024]{2,1,0:T(8,128)(2,1)}, bf16[30,8,1024]{2,1,0:T(8,128)(2,1)}) custom-call(s32[2]{0:T(128)S(1)} %pad_add_fusion.7.where_ref, bf16[24,8,1024]{2,1,0:T(8,128)(2,1)} %get-tuple-element.34.own_ref, bf16[24,8,1024]{2,1,0:T(8,128)(2,1)S(1)} %collective-permute-done.1.part_ref, ...), custom_call_target="tpu_custom_call" | custom-call | flops 23000000512 | bytes 73800000 | tf_op jit(solution)/shard_map/gather_rows/pallas_call | solution.py:35
  25.9 4.3 %collective-permute-start.7 = (bf16[30,8,1024]{2,1,0:T(8,128)(2,1)}, bf16[30,8,1024]{2,1,0:T(8,128)(2,1)S(1)}, u32[]{:S(2)}, u32[]{:S(2)}) collective-permute-start(bf16[30,8,1024]{2,1,0:T(8,128)(2,1)} %get-tuple-element.50), channel_id=1, source_target_pairs={{2,4},{3,5},{4,2},{5,3},{10,12},{11,13},{12,10},{13,11},{18,20},{1... | collective-permute-start | bytes 1474568 | tf_op jit(solution)/shard_map/ppermute | solution.py:571
  30.5 3.7 %gather_rows.5 = (bf16[48,8,1024]{2,1,0:T(8,128)(2,1)}, bf16[30,8,1024]{2,1,0:T(8,128)(2,1)}, bf16[30,8,1024]{2,1,0:T(8,128)(2,1)}) custom-call(s32[2]{0:T(128)S(1)} %pad_add_fusion.7.where_ref, bf16[24,8,1024]{2,1,0:T(8,128)(2,1)} %get-tuple-element.33.own_ref, bf16[24,8,1024]{2,1,0:T(8,128)(2,1)S(1)} %collective-permute-done.part_ref, ...), custom_call_target="tpu_custom_call" | custom-call | flops 23000000512 | bytes 73800000 | tf_op jit(solution)/shard_map/gather_rows/pallas_call | solution.py:35
  34.3 4.3 %collective-permute-start.9 = (bf16[30,8,1024]{2,1,0:T(8,128)(2,1)}, bf16[30,8,1024]{2,1,0:T(8,128)(2,1)S(1)}, u32[]{:S(2)}, u32[]{:S(2)}) collective-permute-start(bf16[30,8,1024]{2,1,0:T(8,128)(2,1)} %get-tuple-element.55), channel_id=1, source_target_pairs={{2,4},{3,5},{4,2},{5,3},{10,12},{11,13},{12,10},{13,11},{18,20},{1... | collective-permute-start | bytes 1474568 | tf_op jit(solution)/shard_map/ppermute | solution.py:571
  38.7 11.8 %filter_rows.3 = (f32[4,8,36,128]{3,2,1,0:T(8,128)}, bf16[3,8,8,1024]{3,2,1,0:T(8,128)(2,1)}, bf16[3,8,8,1024]{3,2,1,0:T(8,128)(2,1)}) custom-call(s32[3]{0:T(128)S(1)} %pad_add_fusion.10.refs_0_, bf16[56,8,1024]{2,1,0:T(8,128)(2,1)} %get-tuple-element.45.refs_1_, bf16[35,8,1024]{2,1,0:T(8,128)(2,1)S(1)} %collective-permute-done.5.refs_2_, ...), custom_call_target="tpu_custom_call" | custom-call | flops 1150000000 | bytes 3690000 | tf_op jit(solution)/shard_map/filter_rows/pallas_call | solution.py:35
  50.5 1.3 %collective-permute-start.8 = (bf16[3,8,8,1024]{3,2,1,0:T(8,128)(2,1)}, bf16[3,8,8,1024]{3,2,1,0:T(8,128)(2,1)S(1)}, u32[]{:S(2)}, u32[]{:S(2)}) collective-permute-start(bf16[3,8,8,1024]{3,2,1,0:T(8,128)(2,1)} %get-tuple-element.53), channel_id=1, source_target_pairs={{0,1},{1,0},{2,3},{3,2},{4,5},{5,4},{6,7},{7,6},{8,9},{9,8},{10,11... | collective-permute-start | bytes 1179656 | tf_op jit(solution)/shard_map/ppermute | solution.py:582
  51.8 11.9 %filter_rows.4 = (bf16[3,8,8,1024]{3,2,1,0:T(8,128)(2,1)}, bf16[3,8,8,1024]{3,2,1,0:T(8,128)(2,1)}) custom-call(s32[3]{0:T(128)S(1)} %pad_add_fusion.9.refs_0_, bf16[48,8,1024]{2,1,0:T(8,128)(2,1)} %get-tuple-element.44.refs_1_, bf16[30,8,1024]{2,1,0:T(8,128)(2,1)S(1)} %collective-permute-done.4.refs_2_, ...), custom_call_target="tpu_custom_call" | custom-call | flops 1150000000 | bytes 3690000 | tf_op jit(solution)/shard_map/filter_rows/pallas_call | solution.py:35
  63.7 0.3 collective-permute-start.11
  64.2 11.8 %filter_rows.5 = (bf16[3,8,8,1024]{3,2,1,0:T(8,128)(2,1)}, bf16[3,5,8,1024]{3,2,1,0:T(8,128)(2,1)}) custom-call(s32[3]{0:T(128)S(1)} %pad_add_fusion.5.refs_0_, bf16[48,8,1024]{2,1,0:T(8,128)(2,1)} %get-tuple-element.42.refs_1_, bf16[30,8,1024]{2,1,0:T(8,128)(2,1)S(1)} %collective-permute-done.3.refs_2_, ...), custom_call_target="tpu_custom_call" | custom-call | flops 1150000000 | bytes 3690000 | tf_op jit(solution)/shard_map/filter_rows/pallas_call | solution.py:35
  76.0 1.3 %collective-permute-start.10 = (bf16[3,5,8,1024]{3,2,1,0:T(8,128)(2,1)}, bf16[3,5,8,1024]{3,2,1,0:T(8,128)(2,1)S(1)}, u32[]{:S(2)}, u32[]{:S(2)}) collective-permute-start(bf16[3,5,8,1024]{3,2,1,0:T(8,128)(2,1)} %get-tuple-element.56), channel_id=1, source_target_pairs={{0,1},{1,0},{2,3},{3,2},{4,5},{5,4},{6,7},{7,6},{8,9},{9,8},{10,11... | collective-permute-start | bytes 737288 | tf_op jit(solution)/shard_map/ppermute | solution.py:582
  77.4 0.8 copy-done.4
  78.1 6.5 %project.2 = (bf16[3,45,8,1024]{3,2,1,0:T(8,128)(2,1)}, f32[3,8,8,1024]{3,2,1,0:T(8,128)}) custom-call(s32[5,2]{1,0:T(8,128)S(1)} %stack.149.refs_0_, bf16[3,8,8,1024]{3,2,1,0:T(8,128)(2,1)} %get-tuple-element.48.refs_1_, bf16[3,8,8,1024]{3,2,1,0:T(8,128)(2,1)} %get-tuple-element.52.refs_2_, bf16[3,8,8,1024]{3,2,1,0:T(8,128)(2,1)} %get-tuple-element.57.refs_3_, ...), custom_call_target="tpu_custom_call" | custom-call | flops 23000000512 | bytes 73800000 | tf_op jit(solution)/shard_map/project/pallas_call | solution.py:35
  84.6 3.3 %project.3 = (bf16[3,45,8,1024]{3,2,1,0:T(8,128)(2,1)}, f32[3,8,8,512]{3,2,1,0:T(8,128)}, f32[3,8,8,512]{3,2,1,0:T(8,128)}) custom-call(s32[1,3]{1,0:T(1,128)S(1)} %add_bitcast_fusion.refs_0_, bf16[3,5,8,1024]{3,2,1,0:T(8,128)(2,1)S(1)} %collective-permute-done.10.refs_1_, bf16[8,45,8,1024]{3,2,1,0:T(8,128)(2,1)} %refs_2_.1, ...), custom_call_target="tpu_custom_call", output_to_operand_aliasing={{0}: (4, {})} | custom-call | flops 23000000512 | bytes 73800000 | tf_op jit(solution)/shard_map/project/pallas_call | solution.py:35
  88.0 3.0 %collective-permute-start.12 = (f32[3,8,8,512]{3,2,1,0:T(8,128)}, f32[3,8,8,512]{3,2,1,0:T(8,128)S(1)}, u32[]{:S(2)}, u32[]{:S(2)}) collective-permute-start(f32[3,8,8,512]{3,2,1,0:T(8,128)} %get-tuple-element.63), channel_id=1, source_target_pairs={{0,8},{8,0},{1,9},{9,1},{2,10},{10,2},{3,11},{11,3},{4,12},{12,4},... | collective-permute-start | bytes 1179656 | tf_op jit(solution)/shard_map/ppermute | solution.py:603
  91.0 1.6 %collective-permute-done.12.other_ref = f32[3,8,8,512]{3,2,1,0:T(8,128)S(1)} collective-permute-done((f32[3,8,8,512]{3,2,1,0:T(8,128)}, f32[3,8,8,512]{3,2,1,0:T(8,128)S(1)}, u32[]{:S(2)}, u32[]{:S(2)}) %collective-permute-start.12) | collective-permute-done | bytes 393248 | tf_op jit(solution)/shard_map/ppermute | solution.py:603
  92.6 1.8 %flux.1 = f32[3,8,8,512]{3,2,1,0:T(8,128)} custom-call(f32[3,8,8,512]{3,2,1,0:T(8,128)} %get-tuple-element.62.keep_ref, f32[3,8,8,512]{3,2,1,0:T(8,128)S(1)} %collective-permute-done.12.other_ref), custom_call_target="tpu_custom_call" | custom-call | tf_op jit(solution)/shard_map/flux/pallas_call | solution.py:35
  (39 shorter events, 1.8 us)
Async XLA Ops:
  0.6 1.4 %copy-start = (f32[8,1024]{1,0:T(8,128)S(1)}, f32[8,1024]{1,0:T(8,128)}, u32[]{:S(2)}) copy-start(f32[8,1024]{1,0:T(8,128)} %param.7) | copy-start | bytes 98308
  0.6 1.5 %copy-start.1 = (s32[8,1024]{1,0:T(8,128)S(1)}, s32[8,1024]{1,0:T(8,128)}, u32[]{:S(2)}) copy-start(s32[8,1024]{1,0:T(8,128)} %param.8) | copy-start | bytes 98308
  0.7 1.5 %copy-start.2 = (s32[8,1024]{1,0:T(8,128)S(1)}, s32[8,1024]{1,0:T(8,128)}, u32[]{:S(2)}) copy-start(s32[8,1024]{1,0:T(8,128)} %param.9) | copy-start | bytes 98308
  2.2 11.5 %collective-permute-start.2 = (bf16[28,8,1024]{2,1,0:T(8,128)(2,1)S(1)}, bf16[28,8,1024]{2,1,0:T(8,128)(2,1)S(1)}, u32[]{:S(2)}, u32[]{:S(2)}) collective-permute-start(bf16[28,8,1024]{2,1,0:T(8,128)(2,1)S(1)} %get-tuple-element.64), channel_id=1, source_target_pairs={{0,1},{1,0},{2,3},{3,2},{4,5},{5,4},{6,7},{7,6},{8,9},{9,8},{10,11... | collective-permute-start | bytes 1376264 | tf_op jit(solution)/shard_map/ppermute | solution.py:554
  3.5 18.6 %collective-permute-start.1 = (bf16[24,8,1024]{2,1,0:T(8,128)(2,1)S(1)}, bf16[24,8,1024]{2,1,0:T(8,128)(2,1)S(1)}, u32[]{:S(2)}, u32[]{:S(2)}) collective-permute-start(bf16[24,8,1024]{2,1,0:T(8,128)(2,1)S(1)} %bitcast.41), channel_id=1, source_target_pairs={{0,1},{1,0},{2,3},{3,2},{4,5},{5,4},{6,7},{7,6},{8,9},{9,8},{10,11... | collective-permute-start | bytes 1179656 | tf_op jit(solution)/shard_map/ppermute | solution.py:554
  3.7 26.8 %collective-permute-start = (bf16[24,8,1024]{2,1,0:T(8,128)(2,1)S(1)}, bf16[24,8,1024]{2,1,0:T(8,128)(2,1)S(1)}, u32[]{:S(2)}, u32[]{:S(2)}) collective-permute-start(bf16[24,8,1024]{2,1,0:T(8,128)(2,1)S(1)} %bitcast.40), channel_id=1, source_target_pairs={{0,1},{1,0},{2,3},{3,2},{4,5},{5,4},{6,7},{7,6},{8,9},{9,8},{10,11... | collective-permute-start | bytes 1179656 | tf_op jit(solution)/shard_map/ppermute | solution.py:554
  17.5 16.8 %collective-permute-start.5 = (bf16[35,8,1024]{2,1,0:T(8,128)(2,1)}, bf16[35,8,1024]{2,1,0:T(8,128)(2,1)S(1)}, u32[]{:S(2)}, u32[]{:S(2)}) collective-permute-start(bf16[35,8,1024]{2,1,0:T(8,128)(2,1)} %get-tuple-element.38), channel_id=1, source_target_pairs={{0,2},{1,3},{2,0},{3,1},{4,6},{5,7},{6,4},{7,5},{8,10},{9,11},{10,... | collective-permute-start | bytes 1720328 | tf_op jit(solution)/shard_map/ppermute | solution.py:570
  17.7 21.0 %collective-permute-start.6 = (bf16[35,8,1024]{2,1,0:T(8,128)(2,1)}, bf16[35,8,1024]{2,1,0:T(8,128)(2,1)S(1)}, u32[]{:S(2)}, u32[]{:S(2)}) collective-permute-start(bf16[35,8,1024]{2,1,0:T(8,128)(2,1)} %get-tuple-element.46), channel_id=1, source_target_pairs={{2,4},{3,5},{4,2},{5,3},{10,12},{11,13},{12,10},{13,11},{18,20},{1... | collective-permute-start | bytes 1720328 | tf_op jit(solution)/shard_map/ppermute | solution.py:571
  25.7 24.8 %collective-permute-start.4 = (bf16[30,8,1024]{2,1,0:T(8,128)(2,1)}, bf16[30,8,1024]{2,1,0:T(8,128)(2,1)S(1)}, u32[]{:S(2)}, u32[]{:S(2)}) collective-permute-start(bf16[30,8,1024]{2,1,0:T(8,128)(2,1)} %get-tuple-element.40), channel_id=1, source_target_pairs={{0,2},{1,3},{2,0},{3,1},{4,6},{5,7},{6,4},{7,5},{8,10},{9,11},{10,... | collective-permute-start | bytes 1474568 | tf_op jit(solution)/shard_map/ppermute | solution.py:570
  25.9 25.9 %collective-permute-start.7 = (bf16[30,8,1024]{2,1,0:T(8,128)(2,1)}, bf16[30,8,1024]{2,1,0:T(8,128)(2,1)S(1)}, u32[]{:S(2)}, u32[]{:S(2)}) collective-permute-start(bf16[30,8,1024]{2,1,0:T(8,128)(2,1)} %get-tuple-element.50), channel_id=1, source_target_pairs={{2,4},{3,5},{4,2},{5,3},{10,12},{11,13},{12,10},{13,11},{18,20},{1... | collective-permute-start | bytes 1474568 | tf_op jit(solution)/shard_map/ppermute | solution.py:571
  34.2 30.0 %collective-permute-start.3 = (bf16[30,8,1024]{2,1,0:T(8,128)(2,1)}, bf16[30,8,1024]{2,1,0:T(8,128)(2,1)S(1)}, u32[]{:S(2)}, u32[]{:S(2)}) collective-permute-start(bf16[30,8,1024]{2,1,0:T(8,128)(2,1)} %get-tuple-element.43), channel_id=1, source_target_pairs={{0,2},{1,3},{2,0},{3,1},{4,6},{5,7},{6,4},{7,5},{8,10},{9,11},{10,... | collective-permute-start | bytes 1474568 | tf_op jit(solution)/shard_map/ppermute | solution.py:570
  34.3 29.9 %collective-permute-start.9 = (bf16[30,8,1024]{2,1,0:T(8,128)(2,1)}, bf16[30,8,1024]{2,1,0:T(8,128)(2,1)S(1)}, u32[]{:S(2)}, u32[]{:S(2)}) collective-permute-start(bf16[30,8,1024]{2,1,0:T(8,128)(2,1)} %get-tuple-element.55), channel_id=1, source_target_pairs={{2,4},{3,5},{4,2},{5,3},{10,12},{11,13},{12,10},{13,11},{18,20},{1... | collective-permute-start | bytes 1474568 | tf_op jit(solution)/shard_map/ppermute | solution.py:571
  50.5 13.7 %collective-permute-start.8 = (bf16[3,8,8,1024]{3,2,1,0:T(8,128)(2,1)}, bf16[3,8,8,1024]{3,2,1,0:T(8,128)(2,1)S(1)}, u32[]{:S(2)}, u32[]{:S(2)}) collective-permute-start(bf16[3,8,8,1024]{3,2,1,0:T(8,128)(2,1)} %get-tuple-element.53), channel_id=1, source_target_pairs={{0,1},{1,0},{2,3},{3,2},{4,5},{5,4},{6,7},{7,6},{8,9},{9,8},{10,11... | collective-permute-start | bytes 1179656 | tf_op jit(solution)/shard_map/ppermute | solution.py:582
  63.7 13.7 %collective-permute-start.11 = (bf16[3,8,8,1024]{3,2,1,0:T(8,128)(2,1)}, bf16[3,8,8,1024]{3,2,1,0:T(8,128)(2,1)S(1)}, u32[]{:S(2)}, u32[]{:S(2)}) collective-permute-start(bf16[3,8,8,1024]{3,2,1,0:T(8,128)(2,1)} %get-tuple-element.58), channel_id=1, source_target_pairs={{0,1},{1,0},{2,3},{3,2},{4,5},{5,4},{6,7},{7,6},{8,9},{9,8},{10,11... | collective-permute-start | bytes 1179656 | tf_op jit(solution)/shard_map/ppermute | solution.py:582
  64.2 11.8 %copy-start.3 = (bf16[3,8,8,1024]{3,2,1,0:T(8,128)(2,1)}, bf16[3,8,8,1024]{3,2,1,0:T(8,128)(2,1)S(1)}, u32[]{:S(2)}) copy-start(bf16[3,8,8,1024]{3,2,1,0:T(8,128)(2,1)S(1)} %collective-permute-done.8.refs_4_) | copy-start | bytes 1179652
  76.0 8.6 %collective-permute-start.10 = (bf16[3,5,8,1024]{3,2,1,0:T(8,128)(2,1)}, bf16[3,5,8,1024]{3,2,1,0:T(8,128)(2,1)S(1)}, u32[]{:S(2)}, u32[]{:S(2)}) collective-permute-start(bf16[3,5,8,1024]{3,2,1,0:T(8,128)(2,1)} %get-tuple-element.56), channel_id=1, source_target_pairs={{0,1},{1,0},{2,3},{3,2},{4,5},{5,4},{6,7},{7,6},{8,9},{9,8},{10,11... | collective-permute-start | bytes 737288 | tf_op jit(solution)/shard_map/ppermute | solution.py:582
  77.4 0.8 copy-start.4
  88.0 4.6 %collective-permute-start.12 = (f32[3,8,8,512]{3,2,1,0:T(8,128)}, f32[3,8,8,512]{3,2,1,0:T(8,128)S(1)}, u32[]{:S(2)}, u32[]{:S(2)}) collective-permute-start(f32[3,8,8,512]{3,2,1,0:T(8,128)} %get-tuple-element.63), channel_id=1, source_target_pairs={{0,8},{8,0},{1,9},{9,1},{2,10},{10,2},{3,11},{11,3},{4,12},{12,4},... | collective-permute-start | bytes 1179656 | tf_op jit(solution)/shard_map/ppermute | solution.py:603

commit v3 on v2

--- a/solution.py
+++ b/solution.py
@@ -265,13 +265,13 @@
         fill(first_ref, 0, ITERS)
         fill(second_ref, ITERS + pair, ITERS)
 
-    if not leads:
-        move_face.wait()
-    get_pair.wait()
-    fill(pair_ref, ITERS, pair)
     if leads:
+        get_pair.wait()
+        fill(pair_ref, ITERS, pair)
         make_faces(face_ref, planes_ref, spare_ref)
         move_face.start()
+    else:
+        move_face.wait()
 
     def weights(r, _):
         for j in range(tiles):
@@ -286,6 +286,9 @@
         return 0
 
     lax.fori_loop(0, total, weights, 0, unroll=4)
+    if not leads:
+        get_pair.wait()
+        fill(pair_ref, ITERS, pair)
 
     def one_field(f, _):
         for step in range(1, ITERS + 1):
@@ -414,10 +417,10 @@
         loads = [pltpu.make_async_copy(start_ref, spare[0], chunk_sems.at[0])]
         start_ref = spare[0]
     else:
-        chunk_bufs = spare
+        chunk_bufs = list(spare) + chunk_refs[-1:]
         loads = [
             pltpu.make_async_copy(chunk_refs[n], chunk_bufs[n], chunk_sems.at[n])
-            for n in range(count)
+            for n in range(count - 1)
         ]
     copies = [
         pltpu.make_async_copy(
@@ -434,7 +437,8 @@
     for fetch in fetches:
         fetch.start()
     for n in range(count):
-        loads[n].wait()
+        if n < len(loads):
+            loads[n].wait()
         if not has_start:
             copies[n].start()
         fetches[n].wait()
@@ -490,11 +494,12 @@
 
     return call(
         body,
-        landed=(1,) if carried else (),
+        landed=(count,),
         out_shape=(jax.ShapeDtypeStruct((fields, levels, rows, cols), BF16),)
         + (amplitude,) * halves,
         in_specs=[whole(pltpu.SMEM)]
-        + [whole() if carried else whole(pl.ANY)] * count
+        + [whole(pl.ANY)] * (count - 1)
+        + [whole()]
         + [whole(pl.ANY)]
         + ([whole(pl.ANY), whole(pl.ANY)] if carried else []),
         out_specs=(whole(pl.ANY),) + (whole(),) * halves,
@@ -504,7 +509,7 @@
         + (
             [pltpu.VMEM((fields, modes, rows, cols), F32)]
             if carried
-            else [pltpu.VMEM(chunk.shape, BF16) for chunk in chunks]
+            else [pltpu.VMEM(chunk.shape, BF16) for chunk in chunks[:-1]]
         ),
         compiler_params=params(24),
         cost_estimate=cost(PROJECT_COST),

time: 94.8 us -> 93.5 us (0.986)
  no operation moved by 1% of the time
where the time goes in v3:
time: 93.5 us; the launch traced here: 93 us
  Pallas kernels  63.6 us (68%)
  starting transfers between devices  22.2 us (24%)
  waiting for transfers between devices  3.64 us (4%)
  local copies, waits for them, and re-layouts  1.41 us (2%)
  other arithmetic  1.35 us (1%)
    pallas_call x10, Pallas kernels, run(): return inner(*pinned)  63.6 us
    ppermute x3, starting transfers between devices, per_device(): second = lax.ppermute(second, 'row', far)  13 us
    ppermute x1, starting transfers between devices, per_device(): other = lax.ppermute(give, 'lev', [(0, 1), (1, 0)])  3.01 us
    ppermute x3, starting transfers between devices, per_device(): returned.append(lax.ppermute(gone, 'row', pairs))  2.9 us
    ppermute x3, starting transfers between devices, per_device(): parts.append(lax.ppermute(piece, 'row', pairs))  2.77 us
    ppermute x3, waiting for transfers between devices, per_device(): parts.append(lax.ppermute(piece, 'row', pairs))  2.05 us
  transfers between devices with their start and end apart: 13, of which 3 were waited for; matrix products, arithmetic and copies ran while one was open for 1% of the time, Pallas kernels for 63%

profile of v3, /device:TPU:11, one launch (start us, length us, event | category | flops | bytes accessed | tf_op | source)
XLA Modules:
  0.0 93.0 jit_solution(12202697321937782363)
XLA Ops:
  0.7 1.3 %constant_dynamic-slice_fusion.1 = (bf16[3,8,8,1024]{3,2,1,0:T(8,128)(2,1)S(1)}, bf16[3,8,8,1024]{3,2,1,0:T(8,128)(2,1)S(1)}, bf16[3,8,8,1024]{3,2,1,0:T(8,128)(2,1)S(1)}) fusion(bf16[3,45,8,1024]{3,2,1,0:T(8,128)(2,1)} %fields_ref.1, s32[]{:T(128)} %select_n.48, s32[]{:T(128)S(6)} %select_n.41, s32[]{:T(128)} %select_n.49), kind=kLoop, calls=%fused_computation.17 | loop fusion | bytes 2359308 | tf_op jit(solution)/shard_map/dynamic_slice | solution.py:555
  2.2 1.3 %collective-permute-start.2 = (bf16[28,8,1024]{2,1,0:T(8,128)(2,1)S(1)}, bf16[28,8,1024]{2,1,0:T(8,128)(2,1)S(1)}, u32[]{:S(2)}, u32[]{:S(2)}) collective-permute-start(bf16[28,8,1024]{2,1,0:T(8,128)(2,1)S(1)} %get-tuple-element.64), channel_id=1, source_target_pairs={{0,1},{1,0},{2,3},{3,2},{4,5},{5,4},{6,7},{7,6},{8,9},{9,8},{10,11... | collective-permute-start | bytes 1376264 | tf_op jit(solution)/shard_map/ppermute | solution.py:559
  3.7 1.2 %collective-permute-start = (bf16[24,8,1024]{2,1,0:T(8,128)(2,1)S(1)}, bf16[24,8,1024]{2,1,0:T(8,128)(2,1)S(1)}, u32[]{:S(2)}, u32[]{:S(2)}) collective-permute-start(bf16[24,8,1024]{2,1,0:T(8,128)(2,1)S(1)} %bitcast.40), channel_id=1, source_target_pairs={{0,1},{1,0},{2,3},{3,2},{4,5},{5,4},{6,7},{7,6},{8,9},{9,8},{10,11... | collective-permute-start | bytes 1179656 | tf_op jit(solution)/shard_map/ppermute | solution.py:559
  5.0 0.6 pad_maximum_fusion.planes_ref
  5.7 5.8 %turn.1 = (bf16[1024,1024]{1,0:T(8,128)(2,1)}, bf16[1024,1024]{1,0:T(8,128)(2,1)}, f32[4,8,1024]{2,1,0:T(8,128)}, bf16[24,8,1024]{2,1,0:T(8,128)(2,1)}, bf16[24,...) custom-call(s32[3]{0:T(128)S(1)} %pad_add_fusion.8.base_ref, bf16[3,45,8,1024]{3,2,1,0:T(8,128)(2,1)} %fields_ref.1, ...), custom_call_target="tpu_custom_call" | custom-call | flops 23000000512 | bytes 73800000 | tf_op jit(solution)/shard_map/turn/pallas_call | solution.py:35
  11.9 1.8 %collective-permute-done.2.part_ref = bf16[28,8,1024]{2,1,0:T(8,128)(2,1)S(1)} collective-permute-done((bf16[28,8,1024]{2,1,0:T(8,128)(2,1)S(1)}, bf16[28,8,1024]{2,1,0:T(8,128)(2,1)S(1)}, u32[]{:S(2)}, u32[]{:S(2)}) %collective-permute-start.2) | collective-permute-done | bytes 458784 | tf_op jit(solution)/shard_map/ppermute | solution.py:559
  13.6 3.9 %gather_rows.3 = (bf16[56,8,1024]{2,1,0:T(8,128)(2,1)}, bf16[35,8,1024]{2,1,0:T(8,128)(2,1)}, bf16[35,8,1024]{2,1,0:T(8,128)(2,1)}) custom-call(s32[2]{0:T(128)S(1)} %pad_add_fusion.7.where_ref, bf16[24,8,1024]{2,1,0:T(8,128)(2,1)} %get-tuple-element.35.own_ref, bf16[28,8,1024]{2,1,0:T(8,128)(2,1)S(1)} %collective-permute-done.2.part_ref, ...), custom_call_target="tpu_custom_call" | custom-call | flops 23000000512 | bytes 73800000 | tf_op jit(solution)/shard_map/gather_rows/pallas_call | solution.py:35
  17.7 4.3 %collective-permute-start.6 = (bf16[35,8,1024]{2,1,0:T(8,128)(2,1)}, bf16[35,8,1024]{2,1,0:T(8,128)(2,1)S(1)}, u32[]{:S(2)}, u32[]{:S(2)}) collective-permute-start(bf16[35,8,1024]{2,1,0:T(8,128)(2,1)} %get-tuple-element.46), channel_id=1, source_target_pairs={{2,4},{3,5},{4,2},{5,3},{10,12},{11,13},{12,10},{13,11},{18,20},{1... | collective-permute-start | bytes 1720328 | tf_op jit(solution)/shard_map/ppermute | solution.py:576
  22.0 3.7 %gather_rows.4 = (bf16[48,8,1024]{2,1,0:T(8,128)(2,1)}, bf16[30,8,1024]{2,1,0:T(8,128)(2,1)}, bf16[30,8,1024]{2,1,0:T(8,128)(2,1)}) custom-call(s32[2]{0:T(128)S(1)} %pad_add_fusion.7.where_ref, bf16[24,8,1024]{2,1,0:T(8,128)(2,1)} %get-tuple-element.34.own_ref, bf16[24,8,1024]{2,1,0:T(8,128)(2,1)S(1)} %collective-permute-done.1.part_ref, ...), custom_call_target="tpu_custom_call" | custom-call | flops 23000000512 | bytes 73800000 | tf_op jit(solution)/shard_map/gather_rows/pallas_call | solution.py:35
  25.9 4.3 %collective-permute-start.7 = (bf16[30,8,1024]{2,1,0:T(8,128)(2,1)}, bf16[30,8,1024]{2,1,0:T(8,128)(2,1)S(1)}, u32[]{:S(2)}, u32[]{:S(2)}) collective-permute-start(bf16[30,8,1024]{2,1,0:T(8,128)(2,1)} %get-tuple-element.50), channel_id=1, source_target_pairs={{2,4},{3,5},{4,2},{5,3},{10,12},{11,13},{12,10},{13,11},{18,20},{1... | collective-permute-start | bytes 1474568 | tf_op jit(solution)/shard_map/ppermute | solution.py:576
  30.2 0.2 collective-permute-done.part_ref
  30.5 3.7 %gather_rows.5 = (bf16[48,8,1024]{2,1,0:T(8,128)(2,1)}, bf16[30,8,1024]{2,1,0:T(8,128)(2,1)}, bf16[30,8,1024]{2,1,0:T(8,128)(2,1)}) custom-call(s32[2]{0:T(128)S(1)} %pad_add_fusion.7.where_ref, bf16[24,8,1024]{2,1,0:T(8,128)(2,1)} %get-tuple-element.33.own_ref, bf16[24,8,1024]{2,1,0:T(8,128)(2,1)S(1)} %collective-permute-done.part_ref, ...), custom_call_target="tpu_custom_call" | custom-call | flops 23000000512 | bytes 73800000 | tf_op jit(solution)/shard_map/gather_rows/pallas_call | solution.py:35
  34.3 4.3 %collective-permute-start.9 = (bf16[30,8,1024]{2,1,0:T(8,128)(2,1)}, bf16[30,8,1024]{2,1,0:T(8,128)(2,1)S(1)}, u32[]{:S(2)}, u32[]{:S(2)}) collective-permute-start(bf16[30,8,1024]{2,1,0:T(8,128)(2,1)} %get-tuple-element.55), channel_id=1, source_target_pairs={{2,4},{3,5},{4,2},{5,3},{10,12},{11,13},{12,10},{13,11},{18,20},{1... | collective-permute-start | bytes 1474568 | tf_op jit(solution)/shard_map/ppermute | solution.py:576
  38.7 11.8 %filter_rows.3 = (f32[4,8,36,128]{3,2,1,0:T(8,128)}, bf16[3,8,8,1024]{3,2,1,0:T(8,128)(2,1)}, bf16[3,8,8,1024]{3,2,1,0:T(8,128)(2,1)}) custom-call(s32[3]{0:T(128)S(1)} %pad_add_fusion.10.refs_0_, bf16[56,8,1024]{2,1,0:T(8,128)(2,1)} %get-tuple-element.45.refs_1_, bf16[35,8,1024]{2,1,0:T(8,128)(2,1)S(1)} %collective-permute-done.5.refs_2_, ...), custom_call_target="tpu_custom_call" | custom-call | flops 1150000000 | bytes 3690000 | tf_op jit(solution)/shard_map/filter_rows/pallas_call | solution.py:35
  50.5 1.3 %collective-permute-start.8 = (bf16[3,8,8,1024]{3,2,1,0:T(8,128)(2,1)}, bf16[3,8,8,1024]{3,2,1,0:T(8,128)(2,1)S(1)}, u32[]{:S(2)}, u32[]{:S(2)}) collective-permute-start(bf16[3,8,8,1024]{3,2,1,0:T(8,128)(2,1)} %get-tuple-element.53), channel_id=1, source_target_pairs={{0,1},{1,0},{2,3},{3,2},{4,5},{5,4},{6,7},{7,6},{8,9},{9,8},{10,11... | collective-permute-start | bytes 1179656 | tf_op jit(solution)/shard_map/ppermute | solution.py:587
  51.8 11.6 %filter_rows.4 = (bf16[3,8,8,1024]{3,2,1,0:T(8,128)(2,1)}, bf16[3,8,8,1024]{3,2,1,0:T(8,128)(2,1)}) custom-call(s32[3]{0:T(128)S(1)} %pad_add_fusion.9.refs_0_, bf16[48,8,1024]{2,1,0:T(8,128)(2,1)} %get-tuple-element.44.refs_1_, bf16[30,8,1024]{2,1,0:T(8,128)(2,1)S(1)} %collective-permute-done.4.refs_2_, ...), custom_call_target="tpu_custom_call" | custom-call | flops 1150000000 | bytes 3690000 | tf_op jit(solution)/shard_map/filter_rows/pallas_call | solution.py:35
  63.4 0.3 collective-permute-start.11
  64.0 11.6 %filter_rows.5 = (bf16[3,8,8,1024]{3,2,1,0:T(8,128)(2,1)}, bf16[3,5,8,1024]{3,2,1,0:T(8,128)(2,1)}) custom-call(s32[3]{0:T(128)S(1)} %pad_add_fusion.5.refs_0_, bf16[48,8,1024]{2,1,0:T(8,128)(2,1)} %get-tuple-element.42.refs_1_, bf16[30,8,1024]{2,1,0:T(8,128)(2,1)S(1)} %collective-permute-done.3.refs_2_, ...), custom_call_target="tpu_custom_call" | custom-call | flops 1150000000 | bytes 3690000 | tf_op jit(solution)/shard_map/filter_rows/pallas_call | solution.py:35
  75.6 1.3 %collective-permute-start.10 = (bf16[3,5,8,1024]{3,2,1,0:T(8,128)(2,1)}, bf16[3,5,8,1024]{3,2,1,0:T(8,128)(2,1)S(1)}, u32[]{:S(2)}, u32[]{:S(2)}) collective-permute-start(bf16[3,5,8,1024]{3,2,1,0:T(8,128)(2,1)} %get-tuple-element.56), channel_id=1, source_target_pairs={{0,1},{1,0},{2,3},{3,2},{4,5},{5,4},{6,7},{7,6},{8,9},{9,8},{10,11... | collective-permute-start | bytes 737288 | tf_op jit(solution)/shard_map/ppermute | solution.py:587
  76.9 6.4 %project.2 = (bf16[3,45,8,1024]{3,2,1,0:T(8,128)(2,1)}, f32[3,8,8,1024]{3,2,1,0:T(8,128)}) custom-call(s32[5,2]{1,0:T(8,128)S(1)} %stack.149.refs_0_, bf16[3,8,8,1024]{3,2,1,0:T(8,128)(2,1)} %get-tuple-element.48.refs_1_, bf16[3,8,8,1024]{3,2,1,0:T(8,128)(2,1)} %get-tuple-element.52.refs_2_, bf16[3,8,8,1024]{3,2,1,0:T(8,128)(2,1)} %get-tuple-element.57.refs_3_, ...), custom_call_target="tpu_custom_call" | custom-call | flops 23000000512 | bytes 73800000 | tf_op jit(solution)/shard_map/project/pallas_call | solution.py:35
  83.3 3.3 %project.3 = (bf16[3,45,8,1024]{3,2,1,0:T(8,128)(2,1)}, f32[3,8,8,512]{3,2,1,0:T(8,128)}, f32[3,8,8,512]{3,2,1,0:T(8,128)}) custom-call(s32[1,3]{1,0:T(1,128)S(1)} %add_bitcast_fusion.refs_0_, bf16[3,5,8,1024]{3,2,1,0:T(8,128)(2,1)S(1)} %collective-permute-done.10.refs_1_, bf16[8,45,8,1024]{3,2,1,0:T(8,128)(2,1)} %refs_2_.1, ...), custom_call_target="tpu_custom_call", output_to_operand_aliasing={{0}: (4, {})} | custom-call | flops 23000000512 | bytes 73800000 | tf_op jit(solution)/shard_map/project/pallas_call | solution.py:35
  86.7 3.0 %collective-permute-start.12 = (f32[3,8,8,512]{3,2,1,0:T(8,128)}, f32[3,8,8,512]{3,2,1,0:T(8,128)S(1)}, u32[]{:S(2)}, u32[]{:S(2)}) collective-permute-start(f32[3,8,8,512]{3,2,1,0:T(8,128)} %get-tuple-element.63), channel_id=1, source_target_pairs={{0,8},{8,0},{1,9},{9,1},{2,10},{10,2},{3,11},{11,3},{4,12},{12,4},... | collective-permute-start | bytes 1179656 | tf_op jit(solution)/shard_map/ppermute | solution.py:608
  89.7 1.6 %collective-permute-done.12.other_ref = f32[3,8,8,512]{3,2,1,0:T(8,128)S(1)} collective-permute-done((f32[3,8,8,512]{3,2,1,0:T(8,128)}, f32[3,8,8,512]{3,2,1,0:T(8,128)S(1)}, u32[]{:S(2)}, u32[]{:S(2)}) %collective-permute-start.12) | collective-permute-done | bytes 393248 | tf_op jit(solution)/shard_map/ppermute | solution.py:608
  91.2 1.8 %flux.1 = f32[3,8,8,512]{3,2,1,0:T(8,128)} custom-call(f32[3,8,8,512]{3,2,1,0:T(8,128)} %get-tuple-element.62.keep_ref, f32[3,8,8,512]{3,2,1,0:T(8,128)S(1)} %collective-permute-done.12.other_ref), custom_call_target="tpu_custom_call" | custom-call | tf_op jit(solution)/shard_map/flux/pallas_call | solution.py:35
  (37 shorter events, 1.6 us)
Async XLA Ops:
  0.6 1.4 %copy-start = (f32[8,1024]{1,0:T(8,128)S(1)}, f32[8,1024]{1,0:T(8,128)}, u32[]{:S(2)}) copy-start(f32[8,1024]{1,0:T(8,128)} %param.7) | copy-start | bytes 98308
  0.6 1.5 %copy-start.1 = (s32[8,1024]{1,0:T(8,128)S(1)}, s32[8,1024]{1,0:T(8,128)}, u32[]{:S(2)}) copy-start(s32[8,1024]{1,0:T(8,128)} %param.8) | copy-start | bytes 98308
  0.7 1.5 %copy-start.2 = (s32[8,1024]{1,0:T(8,128)S(1)}, s32[8,1024]{1,0:T(8,128)}, u32[]{:S(2)}) copy-start(s32[8,1024]{1,0:T(8,128)} %param.9) | copy-start | bytes 98308
  2.2 11.5 %collective-permute-start.2 = (bf16[28,8,1024]{2,1,0:T(8,128)(2,1)S(1)}, bf16[28,8,1024]{2,1,0:T(8,128)(2,1)S(1)}, u32[]{:S(2)}, u32[]{:S(2)}) collective-permute-start(bf16[28,8,1024]{2,1,0:T(8,128)(2,1)S(1)} %get-tuple-element.64), channel_id=1, source_target_pairs={{0,1},{1,0},{2,3},{3,2},{4,5},{5,4},{6,7},{7,6},{8,9},{9,8},{10,11... | collective-permute-start | bytes 1376264 | tf_op jit(solution)/shard_map/ppermute | solution.py:559
  3.5 18.6 %collective-permute-start.1 = (bf16[24,8,1024]{2,1,0:T(8,128)(2,1)S(1)}, bf16[24,8,1024]{2,1,0:T(8,128)(2,1)S(1)}, u32[]{:S(2)}, u32[]{:S(2)}) collective-permute-start(bf16[24,8,1024]{2,1,0:T(8,128)(2,1)S(1)} %bitcast.41), channel_id=1, source_target_pairs={{0,1},{1,0},{2,3},{3,2},{4,5},{5,4},{6,7},{7,6},{8,9},{9,8},{10,11... | collective-permute-start | bytes 1179656 | tf_op jit(solution)/shard_map/ppermute | solution.py:559
  3.7 26.8 %collective-permute-start = (bf16[24,8,1024]{2,1,0:T(8,128)(2,1)S(1)}, bf16[24,8,1024]{2,1,0:T(8,128)(2,1)S(1)}, u32[]{:S(2)}, u32[]{:S(2)}) collective-permute-start(bf16[24,8,1024]{2,1,0:T(8,128)(2,1)S(1)} %bitcast.40), channel_id=1, source_target_pairs={{0,1},{1,0},{2,3},{3,2},{4,5},{5,4},{6,7},{7,6},{8,9},{9,8},{10,11... | collective-permute-start | bytes 1179656 | tf_op jit(solution)/shard_map/ppermute | solution.py:559
  17.5 16.8 %collective-permute-start.5 = (bf16[35,8,1024]{2,1,0:T(8,128)(2,1)}, bf16[35,8,1024]{2,1,0:T(8,128)(2,1)S(1)}, u32[]{:S(2)}, u32[]{:S(2)}) collective-permute-start(bf16[35,8,1024]{2,1,0:T(8,128)(2,1)} %get-tuple-element.38), channel_id=1, source_target_pairs={{0,2},{1,3},{2,0},{3,1},{4,6},{5,7},{6,4},{7,5},{8,10},{9,11},{10,... | collective-permute-start | bytes 1720328 | tf_op jit(solution)/shard_map/ppermute | solution.py:575
  17.7 21.0 %collective-permute-start.6 = (bf16[35,8,1024]{2,1,0:T(8,128)(2,1)}, bf16[35,8,1024]{2,1,0:T(8,128)(2,1)S(1)}, u32[]{:S(2)}, u32[]{:S(2)}) collective-permute-start(bf16[35,8,1024]{2,1,0:T(8,128)(2,1)} %get-tuple-element.46), channel_id=1, source_target_pairs={{2,4},{3,5},{4,2},{5,3},{10,12},{11,13},{12,10},{13,11},{18,20},{1... | collective-permute-start | bytes 1720328 | tf_op jit(solution)/shard_map/ppermute | solution.py:576
  25.7 24.7 %collective-permute-start.4 = (bf16[30,8,1024]{2,1,0:T(8,128)(2,1)}, bf16[30,8,1024]{2,1,0:T(8,128)(2,1)S(1)}, u32[]{:S(2)}, u32[]{:S(2)}) collective-permute-start(bf16[30,8,1024]{2,1,0:T(8,128)(2,1)} %get-tuple-element.40), channel_id=1, source_target_pairs={{0,2},{1,3},{2,0},{3,1},{4,6},{5,7},{6,4},{7,5},{8,10},{9,11},{10,... | collective-permute-start | bytes 1474568 | tf_op jit(solution)/shard_map/ppermute | solution.py:575
  25.9 25.9 %collective-permute-start.7 = (bf16[30,8,1024]{2,1,0:T(8,128)(2,1)}, bf16[30,8,1024]{2,1,0:T(8,128)(2,1)S(1)}, u32[]{:S(2)}, u32[]{:S(2)}) collective-permute-start(bf16[30,8,1024]{2,1,0:T(8,128)(2,1)} %get-tuple-element.50), channel_id=1, source_target_pairs={{2,4},{3,5},{4,2},{5,3},{10,12},{11,13},{12,10},{13,11},{18,20},{1... | collective-permute-start | bytes 1474568 | tf_op jit(solution)/shard_map/ppermute | solution.py:576
  34.2 29.8 %collective-permute-start.3 = (bf16[30,8,1024]{2,1,0:T(8,128)(2,1)}, bf16[30,8,1024]{2,1,0:T(8,128)(2,1)S(1)}, u32[]{:S(2)}, u32[]{:S(2)}) collective-permute-start(bf16[30,8,1024]{2,1,0:T(8,128)(2,1)} %get-tuple-element.43), channel_id=1, source_target_pairs={{0,2},{1,3},{2,0},{3,1},{4,6},{5,7},{6,4},{7,5},{8,10},{9,11},{10,... | collective-permute-start | bytes 1474568 | tf_op jit(solution)/shard_map/ppermute | solution.py:575
  34.3 29.7 %collective-permute-start.9 = (bf16[30,8,1024]{2,1,0:T(8,128)(2,1)}, bf16[30,8,1024]{2,1,0:T(8,128)(2,1)S(1)}, u32[]{:S(2)}, u32[]{:S(2)}) collective-permute-start(bf16[30,8,1024]{2,1,0:T(8,128)(2,1)} %get-tuple-element.55), channel_id=1, source_target_pairs={{2,4},{3,5},{4,2},{5,3},{10,12},{11,13},{12,10},{13,11},{18,20},{1... | collective-permute-start | bytes 1474568 | tf_op jit(solution)/shard_map/ppermute | solution.py:576
  50.5 13.5 %collective-permute-start.8 = (bf16[3,8,8,1024]{3,2,1,0:T(8,128)(2,1)}, bf16[3,8,8,1024]{3,2,1,0:T(8,128)(2,1)S(1)}, u32[]{:S(2)}, u32[]{:S(2)}) collective-permute-start(bf16[3,8,8,1024]{3,2,1,0:T(8,128)(2,1)} %get-tuple-element.53), channel_id=1, source_target_pairs={{0,1},{1,0},{2,3},{3,2},{4,5},{5,4},{6,7},{7,6},{8,9},{9,8},{10,11... | collective-permute-start | bytes 1179656 | tf_op jit(solution)/shard_map/ppermute | solution.py:587
  63.4 13.5 %collective-permute-start.11 = (bf16[3,8,8,1024]{3,2,1,0:T(8,128)(2,1)}, bf16[3,8,8,1024]{3,2,1,0:T(8,128)(2,1)S(1)}, u32[]{:S(2)}, u32[]{:S(2)}) collective-permute-start(bf16[3,8,8,1024]{3,2,1,0:T(8,128)(2,1)} %get-tuple-element.58), channel_id=1, source_target_pairs={{0,1},{1,0},{2,3},{3,2},{4,5},{5,4},{6,7},{7,6},{8,9},{9,8},{10,11... | collective-permute-start | bytes 1179656 | tf_op jit(solution)/shard_map/ppermute | solution.py:587
  64.0 11.6 %copy-start.3 = (bf16[3,8,8,1024]{3,2,1,0:T(8,128)(2,1)}, bf16[3,8,8,1024]{3,2,1,0:T(8,128)(2,1)S(1)}, u32[]{:S(2)}) copy-start(bf16[3,8,8,1024]{3,2,1,0:T(8,128)(2,1)S(1)} %collective-permute-done.8.refs_4_) | copy-start | bytes 1179652
  75.6 7.8 %collective-permute-start.10 = (bf16[3,5,8,1024]{3,2,1,0:T(8,128)(2,1)}, bf16[3,5,8,1024]{3,2,1,0:T(8,128)(2,1)S(1)}, u32[]{:S(2)}, u32[]{:S(2)}) collective-permute-start(bf16[3,5,8,1024]{3,2,1,0:T(8,128)(2,1)} %get-tuple-element.56), channel_id=1, source_target_pairs={{0,1},{1,0},{2,3},{3,2},{4,5},{5,4},{6,7},{7,6},{8,9},{9,8},{10,11... | collective-permute-start | bytes 737288 | tf_op jit(solution)/shard_map/ppermute | solution.py:587
  86.7 4.6 %collective-permute-start.12 = (f32[3,8,8,512]{3,2,1,0:T(8,128)}, f32[3,8,8,512]{3,2,1,0:T(8,128)S(1)}, u32[]{:S(2)}, u32[]{:S(2)}) collective-permute-start(f32[3,8,8,512]{3,2,1,0:T(8,128)} %get-tuple-element.63), channel_id=1, source_target_pairs={{0,8},{8,0},{1,9},{9,1},{2,10},{10,2},{3,11},{11,3},{4,12},{12,4},... | collective-permute-start | bytes 1179656 | tf_op jit(solution)/shard_map/ppermute | solution.py:608
